TPU v7x, 512 devices: a whole 4x8x8 slice. The times are simulated.
512 devices in a mesh: img: 64 (over z, y), freq: 8 (over x, core).
Axes of the slice: x: 4, y: 8, z: 8, core: 2. Of those that a mesh axis runs over, the one named last changes fastest.
Arguments:
- coef: bfloat16 [16384, 1024], P('img', 'freq'), may hold values from -6 to 6
- neighbours: int32 [50, 16384], P(None, 'img'), may hold values from 0 to 16383, as said below
- rot_bin: int32 [50, 16384], P(None, 'img'), may hold values from 0 to 359
- degree: int32 [16384], P('img'), may hold values from 1 to 50
- v_init: float32 [2, 16384], P(None, 'img'), may hold values from -6 to 6
Outputs:
- vector: float32 [2, 16384], P(None, 'img')
- weights: float32 [50, 16384], P(None, 'img')
Inputs may be any that keep to these rules, and one draw needn't show every extreme that they name: `neighbours`: counting devices of 256 consecutive images along img, entry (s, i) names an image on a device at most 8 places from image i's device, cyclically; both distances 8 ahead and behind occur.
All inputs are finite; a program needn't handle non-finite values.
Results may differ from a plain program's by a relative error of at most 0.0004.
Values may be sent and summed in bfloat16 or wider, within the bound.
A program may use at most 64 MiB of HBM per device.

v0:
```python
import math

import jax
import jax.numpy as jnp
from jax import lax
from jax.sharding import PartitionSpec as P

RADIAL = 8
BINS = 360
ITERS = 3


sharpness = 64.0
norm_eps = 1e-05
mean_eps = 1e-06


def passed_along(value, axis, steps):
    count = lax.axis_size(axis)
    pairs = [(source, (source + steps) % count) for source in range(count)]
    return lax.ppermute(value, axis, pairs)


def rotated_terms(own, gathered, theta, first_freq):
    rows, columns = own.shape
    freq_here = columns // (2 * RADIAL)
    own_split = own.reshape(rows, freq_here, 2, RADIAL)
    other = gathered.reshape(gathered.shape[0], rows, freq_here, 2, RADIAL)
    own_turned = jnp.stack([own_split[:, :, 1, :], -own_split[:, :, 0, :]], axis=2)
    p_real = jnp.einsum("ikpq,sikpq->sik", own_split, other, preferred_element_type=jnp.float32)
    p_imag = jnp.einsum("ikpq,sikpq->sik", own_turned, other, preferred_element_type=jnp.float32)
    freq_index = (first_freq + jnp.arange(freq_here)).astype(jnp.float32)
    angle = theta[:, :, None] * freq_index[None, None, :]
    corr = jnp.sum(p_real * jnp.cos(angle) - p_imag * jnp.sin(angle), axis=2)
    other_sq = jnp.einsum("sic,sic->si", gathered, gathered, preferred_element_type=jnp.float32)
    own_sq = jnp.einsum("ic,ic->i", own, own, preferred_element_type=jnp.float32)
    return (corr, other_sq, own_sq)


def direct_coef(coef, span):
    behind_list = []
    ahead_list = []
    for dist in range(1, span + 1):
        behind_list.append(passed_along(coef, "img", dist))
        ahead_list.append(passed_along(coef, "img", -dist))
    return jnp.concatenate(behind_list[::-1] + [coef] + ahead_list, axis=0)


def direct_vector(vector, span):
    behind_list = []
    ahead_list = []
    for dist in range(1, span + 1):
        behind_list.append(passed_along(vector, "img", dist))
        ahead_list.append(passed_along(vector, "img", -dist))
    return jnp.concatenate(behind_list[::-1] + [vector] + ahead_list, axis=1)


def shards(coef, neighbours, rot_bin, degree, v_init):
    rows = coef.shape[0]
    width = coef.shape[1]
    count = lax.axis_size("img")
    span = max(1, count // 8)
    offset = (neighbours // rows - lax.axis_index("img") + span) % count
    local = neighbours % rows
    position = offset * rows + local
    theta = rot_bin.astype(jnp.float32) * (2.0 * math.pi / BINS)
    first_freq = lax.axis_index("freq") * (width // (2 * RADIAL))
    window = direct_coef(coef, span)
    gathered = window[position]
    corr, other_sq, own_sq = rotated_terms(coef, gathered, theta, first_freq)
    corr, other_sq, own_sq = lax.psum((corr, other_sq, own_sq), "freq")
    cos_sim = corr * lax.rsqrt(other_sq + norm_eps) * lax.rsqrt(own_sq + norm_eps)[None, :]
    valid = jnp.arange(neighbours.shape[0])[:, None] < degree[None, :]
    raw = jnp.where(valid, jnp.exp(sharpness * cos_sim), jnp.float32(0.0))
    weights = raw / jnp.sum(raw, axis=0, keepdims=True)
    cosine = jnp.cos(theta)
    sine = jnp.sin(theta)
    total_rows = rows * count
    vector = v_init
    for step in range(ITERS):
        wide = direct_vector(vector, span)
        picked = wide[:, position]
        real = jnp.sum(weights * (cosine * picked[0] - sine * picked[1]), axis=0)
        imag = jnp.sum(weights * (sine * picked[0] + cosine * picked[1]), axis=0)
        image = jnp.stack([real, imag])
        total = lax.psum(jnp.sum(image * image), "img")
        vector = image * lax.rsqrt(total / total_rows + mean_eps)
    return (vector, weights)


def solution(mesh):
    return jax.shard_map(
        shards,
        mesh=mesh,
        in_specs=(P("img", "freq"), P(None, "img"), P(None, "img"), P("img"), P(None, "img")),
        out_specs=(P(None, "img"), P(None, "img")),
        check_vma=False,
    )
```

profile of v0, /device:TPU:2, one launch (start us, length us, event | category | flops | bytes accessed | tf_op | source)
XLA Modules:
  0.0 1122.1 jit_solution(11742855123249713924)
XLA Ops:
  7.2 12.0 %collective-permute-start.30 = (f32[2,256]{1,0:T(2,128)}, f32[2,256]{1,0:T(2,128)S(1)}, u32[]{:S(2)}, u32[]{:S(2)}) collective-permute-start(f32[2,256]{1,0:T(2,128)} %param.9), channel_id=1, source_target_pairs={{0,456},{8,464},{16,472},{24,480},{32,488},{40,496},{48,504},{56,0... | collective-permute-start | bytes 6152 | tf_op jit(solution)/shard_map/ppermute | solution.py:21
  79.1 9.4 collective-permute-start.21
  90.0 8.0 collective-permute-start.22
  146.6 9.6 collective-permute-start.1
  158.1 8.6 collective-permute-start.2
  207.0 7.4 collective-permute-done.6
  216.3 7.5 collective-permute-done.7
  256.5 7.8 collective-permute-start.12
  266.7 26.5 %gather_fusion = bf16[12800,128]{1,0:T(8,128)(2,1)} fusion(bf16[4352,128]{1,0:T(8,128)(2,1)S(1)} %constant_dynamic-update-slice_fusion, s32[13312]{0:T(1024)S(1)} %pad_clamp_fusion), kind=kCustom, calls=%fused_computation | custom fusion | bytes 6604800 | tf_op jit(solution)/shard_map/gather | solution.py:69
  314.8 24.3 %gather_fusion.1 = f32[12800,2]{1,0:T(8,128)} fusion(f32[2,4352]{0,1:T(8,128)S(1)} %copy.66, s32[13312]{0:T(1024)S(1)} %pad_clamp_fusion), kind=kCustom, calls=%fused_computation.1 | custom fusion | bytes 256000 | tf_op jit(solution)/shard_map/gather | solution.py:82
  344.2 38.1 %all-reduce.3.cloned.1.call-done = (f32[256]{0:T(256)}, f32[50,256]{1,0:T(8,128)}, f32[50,256]{1,0:T(8,128)}) async-done(((f32[256]{0:T(256)}, f32[50,256]{1,0:T(8,128)}, f32[50,256]{1,0:T(8,128)}), (f32[256]{0:T(256)}, f32[50,256]{1,0:T(8,128)}, f32[50,256]{1,0:T(8,128)})) %all-reduce.3.cloned.1.call-update) | async-done | bytes 103440 | tf_op jit(solution)/shard_map/psum | solution.py:71
  385.5 144.8 %psum.45 = f32[]{:T(128)} all-reduce(f32[]{:T(128)} %multiply_reduce_fusion.8), channel_id=1, replica_groups=mesh['img'=64,'freq'=8] {'img'}, use_global_device_ids=true, to_apply=%region_8.9 | all-reduce | flops 1 | bytes 8 | tf_op jit(solution)/shard_map/psum | solution.py:86
  560.1 6.9 collective-permute-start.35
  569.4 7.8 collective-permute-start.36
  580.9 11.4 %collective-permute-start.37 = (f32[2,256]{1,0:T(2,128)S(1)}, f32[2,256]{1,0:T(2,128)S(1)}, u32[]{:S(2)}, u32[]{:S(2)}) collective-permute-start(f32[2,256]{1,0:T(2,128)S(1)} %broadcast_multiply_fusion.2), channel_id=1, source_target_pairs={{0,24},{8,32},{16,40},{24,48},{32,56},{40,64},{48,72},{56,80},{64,... | collective-permute-start | bytes 6152 | tf_op jit(solution)/shard_map/ppermute | solution.py:21
  631.2 8.2 collective-permute-start.43
  641.3 24.3 %gather_fusion.2 = f32[12800,2]{1,0:T(8,128)} fusion(f32[2,4352]{0,1:T(8,128)S(1)} %copy.68, s32[13312]{0:T(1024)S(1)} %pad_clamp_fusion), kind=kCustom, calls=%fused_computation.2 | custom fusion | bytes 256000 | tf_op jit(solution)/shard_map/gather | solution.py:82
  671.5 150.7 %psum.46 = f32[]{:T(128)} all-reduce(f32[]{:T(128)} %multiply_reduce_fusion.7), channel_id=1, replica_groups=mesh['img'=64,'freq'=8] {'img'}, use_global_device_ids=true, to_apply=%region_12.13 | all-reduce | flops 1 | bytes 8 | tf_op jit(solution)/shard_map/psum | solution.py:86
  851.9 6.8 collective-permute-start.51
  861.3 7.8 collective-permute-start.52
  872.7 11.4 %collective-permute-start.53 = (f32[2,256]{1,0:T(2,128)S(1)}, f32[2,256]{1,0:T(2,128)S(1)}, u32[]{:S(2)}, u32[]{:S(2)}) collective-permute-start(f32[2,256]{1,0:T(2,128)S(1)} %broadcast_multiply_fusion.1), channel_id=1, source_target_pairs={{0,24},{8,32},{16,40},{24,48},{32,56},{40,64},{48,72},{56,80},{64,... | collective-permute-start | bytes 6152 | tf_op jit(solution)/shard_map/ppermute | solution.py:21
  923.0 8.0 collective-permute-start.59
  933.1 24.3 %gather_fusion.3 = f32[12800,2]{1,0:T(8,128)} fusion(f32[2,4352]{0,1:T(8,128)S(1)} %copy.70, s32[13312]{0:T(1024)S(1)} %pad_clamp_fusion), kind=kCustom, calls=%fused_computation.3 | custom fusion | bytes 256000 | tf_op jit(solution)/shard_map/gather | solution.py:82
  963.3 150.7 %psum.47 = f32[]{:T(128)} all-reduce(f32[]{:T(128)} %multiply_reduce_fusion.6), channel_id=1, replica_groups=mesh['img'=64,'freq'=8] {'img'}, use_global_device_ids=true, to_apply=%region_16.17 | all-reduce | flops 1 | bytes 8 | tf_op jit(solution)/shard_map/psum | solution.py:86
  (228 shorter events, 383.1 us)
Async XLA Ops:
  7.2 375.1 %all-reduce.3.cloned.1.call-start = ((), (), s32[]{:S(2)}) async-start(), calls=%async_computation | async-start | bytes 231424 | tf_op jit(solution)/shard_map/psum | solution.py:71
  7.2 131.6 %collective-permute-start.30 = (f32[2,256]{1,0:T(2,128)}, f32[2,256]{1,0:T(2,128)S(1)}, u32[]{:S(2)}, u32[]{:S(2)}) collective-permute-start(f32[2,256]{1,0:T(2,128)} %param.9), channel_id=1, source_target_pairs={{0,456},{8,464},{16,472},{24,480},{32,488},{40,496},{48,504},{56,0... | collective-permute-start | bytes 6152 | tf_op jit(solution)/shard_map/ppermute | solution.py:21
  19.2 115.3 %collective-permute-start.29 = (f32[2,256]{1,0:T(2,128)}, f32[2,256]{1,0:T(2,128)S(1)}, u32[]{:S(2)}, u32[]{:S(2)}) collective-permute-start(f32[2,256]{1,0:T(2,128)} %param.9), channel_id=1, source_target_pairs={{0,464},{8,472},{16,480},{24,488},{32,496},{40,504},{48,0},{56,8},... | collective-permute-start | bytes 6152 | tf_op jit(solution)/shard_map/ppermute | solution.py:21
  23.7 108.9 %collective-permute-start.28 = (f32[2,256]{1,0:T(2,128)}, f32[2,256]{1,0:T(2,128)S(1)}, u32[]{:S(2)}, u32[]{:S(2)}) collective-permute-start(f32[2,256]{1,0:T(2,128)} %param.9), channel_id=1, source_target_pairs={{0,472},{8,480},{16,488},{24,496},{32,504},{40,0},{48,8},{56,16},{... | collective-permute-start | bytes 6152 | tf_op jit(solution)/shard_map/ppermute | solution.py:21
  28.6 102.0 %collective-permute-start.27 = (f32[2,256]{1,0:T(2,128)}, f32[2,256]{1,0:T(2,128)S(1)}, u32[]{:S(2)}, u32[]{:S(2)}) collective-permute-start(f32[2,256]{1,0:T(2,128)} %param.9), channel_id=1, source_target_pairs={{0,480},{8,488},{16,496},{24,504},{32,0},{40,8},{48,16},{56,24},{6... | collective-permute-start | bytes 6152 | tf_op jit(solution)/shard_map/ppermute | solution.py:21
  67.4 11.7 %collective-permute-start.20 = (f32[2,256]{1,0:T(2,128)}, f32[2,256]{1,0:T(2,128)S(1)}, u32[]{:S(2)}, u32[]{:S(2)}) collective-permute-start(f32[2,256]{1,0:T(2,128)} %param.9), channel_id=1, source_target_pairs={{0,32},{8,40},{16,48},{24,56},{32,64},{40,72},{48,80},{56,88},{64,... | collective-permute-start | bytes 6152 | tf_op jit(solution)/shard_map/ppermute | solution.py:21
  128.7 184.8 %collective-permute-start.31 = (f32[2,256]{1,0:T(2,128)}, f32[2,256]{1,0:T(2,128)}, u32[]{:S(2)}, u32[]{:S(2)}) collective-permute-start(f32[2,256]{1,0:T(2,128)} %param.9), channel_id=1, source_target_pairs={{0,448},{8,456},{16,464},{24,472},{32,480},{40,488},{48,496},{56,5... | collective-permute-start | bytes 6152 | tf_op jit(solution)/shard_map/ppermute | solution.py:21
  130.6 136.1 %collective-permute-start.15 = (bf16[256,128]{1,0:T(8,128)(2,1)S(1)}, bf16[256,128]{1,0:T(8,128)(2,1)S(1)}, u32[]{:S(2)}, u32[]{:S(2)}) collective-permute-start(bf16[256,128]{1,0:T(8,128)(2,1)S(1)} %copy-done.2), channel_id=1, source_target_pairs={{0,448},{8,456},{16,464},{24,472},{32,480},{40,488},{48,496},{56,5... | collective-permute-start | bytes 196616 | tf_op jit(solution)/shard_map/ppermute | solution.py:21
  132.6 134.1 %collective-permute-start.14 = (bf16[256,128]{1,0:T(8,128)(2,1)S(1)}, bf16[256,128]{1,0:T(8,128)(2,1)S(1)}, u32[]{:S(2)}, u32[]{:S(2)}) collective-permute-start(bf16[256,128]{1,0:T(8,128)(2,1)S(1)} %copy-done.2), channel_id=1, source_target_pairs={{0,456},{8,464},{16,472},{24,480},{32,488},{40,496},{48,504},{56,0... | collective-permute-start | bytes 196616 | tf_op jit(solution)/shard_map/ppermute | solution.py:21
  134.5 132.1 %collective-permute-start.13 = (bf16[256,128]{1,0:T(8,128)(2,1)S(1)}, bf16[256,128]{1,0:T(8,128)(2,1)S(1)}, u32[]{:S(2)}, u32[]{:S(2)}) collective-permute-start(bf16[256,128]{1,0:T(8,128)(2,1)S(1)} %copy-done.2), channel_id=1, source_target_pairs={{0,464},{8,472},{16,480},{24,488},{32,496},{40,504},{48,0},{56,8},... | collective-permute-start | bytes 196616 | tf_op jit(solution)/shard_map/ppermute | solution.py:21
  158.1 11.8 %collective-permute-start.2 = (bf16[256,128]{1,0:T(8,128)(2,1)S(1)}, bf16[256,128]{1,0:T(8,128)(2,1)S(1)}, u32[]{:S(2)}, u32[]{:S(2)}) collective-permute-start(bf16[256,128]{1,0:T(8,128)(2,1)S(1)} %copy-done.2), channel_id=1, source_target_pairs={{0,48},{8,56},{16,64},{24,72},{32,80},{40,88},{48,96},{56,104},{64... | collective-permute-start | bytes 196616 | tf_op jit(solution)/shard_map/ppermute | solution.py:21
  180.5 12.3 %collective-permute-start.4 = (bf16[256,128]{1,0:T(8,128)(2,1)S(1)}, bf16[256,128]{1,0:T(8,128)(2,1)S(1)}, u32[]{:S(2)}, u32[]{:S(2)}) collective-permute-start(bf16[256,128]{1,0:T(8,128)(2,1)S(1)} %copy-done.2), channel_id=1, source_target_pairs={{0,32},{8,40},{16,48},{24,56},{32,64},{40,72},{48,80},{56,88},{64,... | collective-permute-start | bytes 196616 | tf_op jit(solution)/shard_map/ppermute | solution.py:21
  531.1 12.9 %collective-permute-start.32 = (f32[2,256]{1,0:T(2,128)S(1)}, f32[2,256]{1,0:T(2,128)S(1)}, u32[]{:S(2)}, u32[]{:S(2)}) collective-permute-start(f32[2,256]{1,0:T(2,128)S(1)} %broadcast_multiply_fusion.2), channel_id=1, source_target_pairs={{0,64},{8,72},{16,80},{24,88},{32,96},{40,104},{48,112},{56,120},{... | collective-permute-start | bytes 6152 | tf_op jit(solution)/shard_map/ppermute | solution.py:21
  533.0 107.6 %collective-permute-start.47 = (f32[2,256]{1,0:T(2,128)S(1)}, f32[2,256]{1,0:T(2,128)S(1)}, u32[]{:S(2)}, u32[]{:S(2)}) collective-permute-start(f32[2,256]{1,0:T(2,128)S(1)} %broadcast_multiply_fusion.2), channel_id=1, source_target_pairs={{0,448},{8,456},{16,464},{24,472},{32,480},{40,488},{48,496},{56,5... | collective-permute-start | bytes 6152 | tf_op jit(solution)/shard_map/ppermute | solution.py:21
  538.1 102.5 %collective-permute-start.46 = (f32[2,256]{1,0:T(2,128)S(1)}, f32[2,256]{1,0:T(2,128)S(1)}, u32[]{:S(2)}, u32[]{:S(2)}) collective-permute-start(f32[2,256]{1,0:T(2,128)S(1)} %broadcast_multiply_fusion.2), channel_id=1, source_target_pairs={{0,456},{8,464},{16,472},{24,480},{32,488},{40,496},{48,504},{56,0... | collective-permute-start | bytes 6152 | tf_op jit(solution)/shard_map/ppermute | solution.py:21
  540.1 100.5 %collective-permute-start.45 = (f32[2,256]{1,0:T(2,128)S(1)}, f32[2,256]{1,0:T(2,128)S(1)}, u32[]{:S(2)}, u32[]{:S(2)}) collective-permute-start(f32[2,256]{1,0:T(2,128)S(1)} %broadcast_multiply_fusion.2), channel_id=1, source_target_pairs={{0,464},{8,472},{16,480},{24,488},{32,496},{40,504},{48,0},{56,8},... | collective-permute-start | bytes 6152 | tf_op jit(solution)/shard_map/ppermute | solution.py:21
  542.0 98.6 %collective-permute-start.44 = (f32[2,256]{1,0:T(2,128)S(1)}, f32[2,256]{1,0:T(2,128)S(1)}, u32[]{:S(2)}, u32[]{:S(2)}) collective-permute-start(f32[2,256]{1,0:T(2,128)S(1)} %broadcast_multiply_fusion.2), channel_id=1, source_target_pairs={{0,472},{8,480},{16,488},{24,496},{32,504},{40,0},{48,8},{56,16},{... | collective-permute-start | bytes 6152 | tf_op jit(solution)/shard_map/ppermute | solution.py:21
  580.9 12.7 %collective-permute-start.37 = (f32[2,256]{1,0:T(2,128)S(1)}, f32[2,256]{1,0:T(2,128)S(1)}, u32[]{:S(2)}, u32[]{:S(2)}) collective-permute-start(f32[2,256]{1,0:T(2,128)S(1)} %broadcast_multiply_fusion.2), channel_id=1, source_target_pairs={{0,24},{8,32},{16,40},{24,48},{32,56},{40,64},{48,72},{56,80},{64,... | collective-permute-start | bytes 6152 | tf_op jit(solution)/shard_map/ppermute | solution.py:21
  822.9 12.9 %collective-permute-start.48 = (f32[2,256]{1,0:T(2,128)S(1)}, f32[2,256]{1,0:T(2,128)S(1)}, u32[]{:S(2)}, u32[]{:S(2)}) collective-permute-start(f32[2,256]{1,0:T(2,128)S(1)} %broadcast_multiply_fusion.1), channel_id=1, source_target_pairs={{0,64},{8,72},{16,80},{24,88},{32,96},{40,104},{48,112},{56,120},{... | collective-permute-start | bytes 6152 | tf_op jit(solution)/shard_map/ppermute | solution.py:21
  824.8 107.6 %collective-permute-start.63 = (f32[2,256]{1,0:T(2,128)S(1)}, f32[2,256]{1,0:T(2,128)S(1)}, u32[]{:S(2)}, u32[]{:S(2)}) collective-permute-start(f32[2,256]{1,0:T(2,128)S(1)} %broadcast_multiply_fusion.1), channel_id=1, source_target_pairs={{0,448},{8,456},{16,464},{24,472},{32,480},{40,488},{48,496},{56,5... | collective-permute-start | bytes 6152 | tf_op jit(solution)/shard_map/ppermute | solution.py:21
  829.9 102.5 %collective-permute-start.62 = (f32[2,256]{1,0:T(2,128)S(1)}, f32[2,256]{1,0:T(2,128)S(1)}, u32[]{:S(2)}, u32[]{:S(2)}) collective-permute-start(f32[2,256]{1,0:T(2,128)S(1)} %broadcast_multiply_fusion.1), channel_id=1, source_target_pairs={{0,456},{8,464},{16,472},{24,480},{32,488},{40,496},{48,504},{56,0... | collective-permute-start | bytes 6152 | tf_op jit(solution)/shard_map/ppermute | solution.py:21
  831.9 100.5 %collective-permute-start.61 = (f32[2,256]{1,0:T(2,128)S(1)}, f32[2,256]{1,0:T(2,128)S(1)}, u32[]{:S(2)}, u32[]{:S(2)}) collective-permute-start(f32[2,256]{1,0:T(2,128)S(1)} %broadcast_multiply_fusion.1), channel_id=1, source_target_pairs={{0,464},{8,472},{16,480},{24,488},{32,496},{40,504},{48,0},{56,8},... | collective-permute-start | bytes 6152 | tf_op jit(solution)/shard_map/ppermute | solution.py:21
  833.8 98.6 %collective-permute-start.60 = (f32[2,256]{1,0:T(2,128)S(1)}, f32[2,256]{1,0:T(2,128)S(1)}, u32[]{:S(2)}, u32[]{:S(2)}) collective-permute-start(f32[2,256]{1,0:T(2,128)S(1)} %broadcast_multiply_fusion.1), channel_id=1, source_target_pairs={{0,472},{8,480},{16,488},{24,496},{32,504},{40,0},{48,8},{56,16},{... | collective-permute-start | bytes 6152 | tf_op jit(solution)/shard_map/ppermute | solution.py:21
  872.7 12.7 %collective-permute-start.53 = (f32[2,256]{1,0:T(2,128)S(1)}, f32[2,256]{1,0:T(2,128)S(1)}, u32[]{:S(2)}, u32[]{:S(2)}) collective-permute-start(f32[2,256]{1,0:T(2,128)S(1)} %broadcast_multiply_fusion.1), channel_id=1, source_target_pairs={{0,24},{8,32},{16,40},{24,48},{32,56},{40,64},{48,72},{56,80},{64,... | collective-permute-start | bytes 6152 | tf_op jit(solution)/shard_map/ppermute | solution.py:21
  (48 other events, 1161.1 us)
Sparse Core Ops, SparseCore 0:
  313.5 68.6 all-reduce.2
where the time goes:
time: 1120 us
  blocking collectives  446 us (40%)
  starting transfers between devices  304 us (27%)
  waiting for transfers between devices  205 us (18%)
  local copies, waits for them, and re-layouts  131 us (12%)
  other arithmetic  18.6 us (2%)
  between operations  17.1 us (2%)
    psum x3, blocking collectives, shards(): total = lax.psum(jnp.sum(image * image), 'img')  446 us
    ppermute x64, starting transfers between devices, passed_along(): return lax.ppermute(value, axis, pairs)  304 us
    ppermute x64, waiting for transfers between devices, passed_along(): return lax.ppermute(value, axis, pairs)  167 us
    gather x6, local copies, waits for them, and re-layouts, shards(): picked = wide[:, position]  88 us
    psum x1, waiting for transfers between devices, shards(): corr, other_sq, own_sq = lax.psum((corr, other_sq, own_sq), 'freq')  38.1 us
    gather x2, local copies, waits for them, and re-layouts, shards(): gathered = window[position]  32.2 us
  transfers between devices with their start and end apart: 65, of which 46 were waited for; matrix products, arithmetic and copies ran while one was open for 8% of the time, Pallas kernels for 0%

commit v1 on v0

v1 whole, which is shorter than its diff:
```python
import math

import jax
import jax.numpy as jnp
from jax import lax
from jax.experimental import pallas as pl
from jax.experimental.pallas import tpu as pltpu
from jax.sharding import PartitionSpec as P

RADIAL = 8
BINS = 360
ITERS = 3
LANES = 128
SPAN = 8
BLOCKS = 2 * SPAN + 1
PIECE = 24
SQ_ROW = 104

sharpness = 64.0
norm_eps = 1e-05
mean_eps = 1e-06

MESH = pl.DeviceIdType.MESH
STEPS = [sign * dist for dist in range(SPAN, 0, -1) for sign in (1, -1)]


def cos_sin_turns(units):
    turns = jnp.floor((units + 0.5) * (1.0 / BINS))
    rest = units - turns * BINS
    quarter = jnp.floor((rest + 45.0) * (1.0 / 90.0) + 1e-3)
    x = (rest - quarter * 90.0) * (math.pi / 180.0)
    y = x * x
    s = x * (1.0 + y * (-1.0 / 6 + y * (1.0 / 120 + y * (-1.0 / 5040 + y * (1.0 / 362880)))))
    c = 1.0 + y * (-0.5 + y * (1.0 / 24 + y * (-1.0 / 720 + y * (1.0 / 40320))))
    odd = (quarter == 1.0) | (quarter == 3.0)
    cos = jnp.where(odd, s, c)
    sin = jnp.where(odd, c, s)
    cos = jnp.where((quarter == 1.0) | (quarter == 2.0), -cos, cos)
    sin = jnp.where((quarter == 2.0) | (quarter == 3.0), -sin, sin)
    return cos, sin


def img_at(me, step, count):
    return {"img": lax.rem(me + (step + count), count)}


def greet(targets):
    barrier = pltpu.get_barrier_semaphore()
    for target in targets:
        pl.semaphore_signal(barrier, inc=1, device_id=target, device_id_type=MESH)
    pl.semaphore_wait(barrier, len(targets))


def window_kernel(count, coef_ref, vec_ref, win_ref, vwin_ref, send, recv, vsend, vrecv, local):
    me = lax.axis_index("img")
    greet([img_at(me, step, count) for step in STEPS])
    copies = []
    for n, step in enumerate(STEPS):
        slot = SPAN - step
        for src, dst, ss, rs in ((coef_ref, win_ref, send, recv), (vec_ref, vwin_ref, vsend, vrecv)):
            copy = pltpu.make_async_remote_copy(
                src_ref=src, dst_ref=dst.at[slot], send_sem=ss.at[n], recv_sem=rs.at[n],
                device_id=img_at(me, step, count), device_id_type=MESH)
            copy.start()
            copies.append(copy)
    own = pltpu.make_async_copy(coef_ref, win_ref.at[SPAN], local.at[0])
    own_vec = pltpu.make_async_copy(vec_ref, vwin_ref.at[SPAN], local.at[1])
    own.start()
    own_vec.start()
    own.wait()
    own_vec.wait()
    for copy in copies:
        copy.wait()


def window_call(coef, vec, count):
    rows, width = coef.shape
    n = len(STEPS)
    return pl.pallas_call(
        lambda *refs: window_kernel(count, *refs),
        out_shape=(jax.ShapeDtypeStruct((BLOCKS, rows, width), coef.dtype),
                   jax.ShapeDtypeStruct((BLOCKS, 8, LANES), jnp.float32)),
        in_specs=[pl.BlockSpec(memory_space=pltpu.VMEM)] * 2,
        out_specs=(pl.BlockSpec(memory_space=pltpu.VMEM),) * 2,
        scratch_shapes=[pltpu.SemaphoreType.DMA((n,))] * 4 + [pltpu.SemaphoreType.DMA((2,))],
        compiler_params=pltpu.CompilerParams(collective_id=0, has_side_effects=True),
        name="window",
    )(coef, vec)


def split_exact(value):
    high = value.astype(jnp.bfloat16)
    low = (value - high.astype(jnp.float32)).astype(jnp.bfloat16)
    return jnp.concatenate([high, low], axis=1)


def lane_sums(select, value):
    return lax.dot_general(select, value, (((1,), (1,)), ((), ())), preferred_element_type=jnp.float32)


def pair_kernel(slots, idx_ref, win_ref, bins_ref, out_ref, wide, turned, *tiles):
    rows = win_ref.shape[1]
    first = lax.axis_index("freq") * (LANES // (2 * RADIAL))
    lane = lax.broadcasted_iota(jnp.int32, (8, 2 * LANES), 1)
    sub = lax.broadcasted_iota(jnp.int32, (8, 2 * LANES), 0)
    select = jnp.where((lane % LANES) // (2 * RADIAL) == sub, 1.0, 0.0).astype(jnp.bfloat16)
    ones = jnp.ones((8, 2 * LANES), jnp.bfloat16)
    freq = (first + lax.broadcasted_iota(jnp.int32, (8, LANES), 0)).astype(jnp.float32)
    out_ref[...] = jnp.zeros_like(out_ref)

    for block in range(BLOCKS):
        part = win_ref[block].astype(jnp.float32)
        wide[block * rows:(block + 1) * rows, :] = part
        for half in range(rows // LANES):
            piece = part[half * LANES:(half + 1) * LANES]
            at = SQ_ROW + block * 2 + half
            out_ref[at:at + 1, :] = lane_sums(ones, split_exact(piece * piece))[0:1]

    own = wide[SPAN * rows:(SPAN + 1) * rows, :]
    column = lax.broadcasted_iota(jnp.int32, own.shape, 1)
    turned[...] = jnp.where(column % (2 * RADIAL) < RADIAL,
                            pltpu.roll(own, LANES - RADIAL, 1), -pltpu.roll(own, RADIAL, 1))

    per = len(tiles)

    def body(step, carry):
        for n in range(per):
            row = step * per + n
            tile = tiles[n]
            for pair in range(LANES):
                tile[pair:pair + 1, :] = wide[pl.ds(idx_ref[row, pair], 1), :]
        for n in range(per):
            row = step * per + n
            half = n % 2
            other = tiles[n][...]
            base = SPAN * rows + half * LANES
            real = split_exact(wide[base:base + LANES, :] * other)
            imag = split_exact(turned[half * LANES:(half + 1) * LANES, :] * other)
            sums = lane_sums(select, jnp.concatenate([real, imag], axis=0))
            units = bins_ref[pl.ds(row, 1), :].astype(jnp.float32) * freq
            cos, sin = cos_sin_turns(units)
            terms = sums[:, :LANES] * cos - sums[:, LANES:] * sin
            out_ref[pl.ds(row, 1), :] = jnp.sum(terms, axis=0, keepdims=True)
        return carry

    lax.fori_loop(0, 2 * slots // per, body, 0)


def pair_call(idx, window, bins, slots):
    blocks, rows, width = window.shape
    vmem = pl.BlockSpec(memory_space=pltpu.VMEM)
    return pl.pallas_call(
        lambda *refs: pair_kernel(slots, *refs),
        out_shape=jax.ShapeDtypeStruct((8 * PIECE, LANES), jnp.float32),
        in_specs=[pl.BlockSpec(memory_space=pltpu.SMEM), vmem, vmem],
        out_specs=vmem,
        scratch_shapes=[pltpu.VMEM((blocks * rows, width), jnp.float32),
                        pltpu.VMEM((rows, width), jnp.float32)]
        + [pltpu.VMEM((LANES, LANES), jnp.float32)] * 4,
        name="pairs",
    )(idx, window, bins)


def pick(low, high, sources):
    count = len(low)
    found = None
    for row in range(BLOCKS * 2):
        wide = [jnp.broadcast_to(part, (8, LANES)) for part in sources(row)]
        got = [[jnp.take_along_axis(part, low[m], axis=1, mode="promise_in_bounds") for m in range(count)]
               for part in wide]
        if found is None:
            found = got
        else:
            hit = [high[m] == row for m in range(count)]
            found = [[jnp.where(hit[m], new[m], old[m]) for m in range(count)] for new, old in zip(got, found)]
    return found


def fold(total):
    total = total + pltpu.roll(total, 4, 0)
    return total + pltpu.roll(total, 2, 0)


def power_kernel(count, groups, part_ref, vwin_ref, idx_ref, bins_ref, deg_ref, weights_ref, vec_ref,
                 rs_buf, ag_buf, vec1, vec2, ynorm, znorm,
                 rs_send, rs_recv, ag_send, ag_recv, v_send, v_recv, n_send, n_recv):
    me = lax.axis_index("img")
    mine = lax.axis_index("freq")
    y, z = lax.rem(me, 8), me // 8
    freq_at = lambda q: {"freq": lax.rem(mine + q, 8)}
    y_at = lambda q: {"img": z * 8 + lax.rem(y + q, 8)}
    z_at = lambda q: {"img": lax.rem(z + q, 8) * 8 + y}
    greet([img_at(me, step, count) for step in STEPS] + [freq_at(q) for q in range(1, 8)]
          + [y_at(q) for q in range(1, 8)] + [z_at(q) for q in range(1, 8)])

    copies = []
    for q in range(1, 8):
        copy = pltpu.make_async_remote_copy(
            src_ref=part_ref.at[lax.rem(mine + q, 8)], dst_ref=rs_buf.at[q - 1],
            send_sem=rs_send.at[q - 1], recv_sem=rs_recv.at[q - 1], device_id=freq_at(q), device_id_type=MESH)
        copy.start()
        copies.append(copy)
    sub = lax.broadcasted_iota(jnp.int32, (8, LANES), 0)
    low, high, cosine, sine, valid = [], [], [], [], []
    for m in range(groups):
        idx = idx_ref[m * 8:(m + 1) * 8, :]
        low.append(idx & (LANES - 1))
        high.append(idx >> 7)
        cos, sin = cos_sin_turns(bins_ref[m * 8:(m + 1) * 8, :].astype(jnp.float32))
        cosine.append(cos)
        sine.append(sin)
        valid.append((sub // 2 + m * 4) < deg_ref[...])
    for copy in copies:
        copy.wait()
    total = part_ref[mine]
    for q in range(7):
        total = total + rs_buf[q]
    ag_buf[mine] = total
    copies = []
    for q in range(1, 8):
        copy = pltpu.make_async_remote_copy(
            src_ref=ag_buf.at[mine], dst_ref=ag_buf.at[mine],
            send_sem=ag_send.at[q - 1], recv_sem=ag_recv.at[q - 1], device_id=freq_at(q), device_id_type=MESH)
        copy.start()
        copies.append(copy)
    for copy in copies:
        copy.wait()

    def ag_row(row, size):
        piece, at = row // PIECE, row % PIECE
        return ag_buf[piece, at:at + size, :]

    sq_row = lambda row: ag_row(SQ_ROW + row, 1)
    own = jnp.where(sub % 2 == 0, sq_row(2 * SPAN), sq_row(2 * SPAN + 1))
    own_root = lax.rsqrt(own + norm_eps)
    (other_sq,) = pick(low, high, lambda row: (sq_row(row),))
    raw = []
    for m in range(groups):
        cos_sim = ag_row(m * 8, 8) * lax.rsqrt(other_sq[m] + norm_eps) * own_root
        raw.append(jnp.where(valid[m], jnp.exp(sharpness * cos_sim), 0.0))
    denom = raw[0]
    for m in range(1, groups):
        denom = denom + raw[m]
    denom = fold(denom)
    for m in range(groups):
        weight = raw[m] / denom
        weights_ref[m * 8:(m + 1) * 8, :] = weight
        cosine[m] = weight * cosine[m]
        sine[m] = weight * sine[m]

    norms = []
    source = vwin_ref
    for step in range(ITERS):
        here = source
        sources = lambda row: (here[row // 2, row % 2:row % 2 + 1, :], here[row // 2, 2 + row % 2:3 + row % 2, :])
        real_at, imag_at = pick(low, high, sources)
        real = imag = jnp.zeros((8, LANES), jnp.float32)
        for m in range(groups):
            real = real + (cosine[m] * real_at[m] - sine[m] * imag_at[m])
            imag = imag + (sine[m] * real_at[m] + cosine[m] * imag_at[m])
        real, imag = fold(real), fold(imag)
        square = real * real + imag * imag
        norms.append(square + pltpu.roll(square, 1, 0))
        packed = jnp.where(sub % 4 < 2, real, imag)
        if step < ITERS - 1:
            into = (vec1, vec2)[step]
            into[SPAN] = packed
            copies = []
            for n, hop in enumerate(STEPS):
                copy = pltpu.make_async_remote_copy(
                    src_ref=into.at[SPAN], dst_ref=into.at[SPAN - hop], send_sem=v_send.at[step, n],
                    recv_sem=v_recv.at[step, n], device_id=img_at(me, hop, count), device_id_type=MESH)
                copy.start()
                copies.append(copy)
            for copy in copies:
                copy.wait()
            source = into

    message = jnp.where(sub == 0, norms[0], jnp.where(sub == 1, norms[1], norms[2]))
    for axis, (buf, where) in enumerate(((ynorm, y_at), (znorm, z_at))):
        buf[7] = message
        copies = []
        for q in range(1, 8):
            copy = pltpu.make_async_remote_copy(
                src_ref=buf.at[7], dst_ref=buf.at[q - 1], send_sem=n_send.at[axis, q - 1],
                recv_sem=n_recv.at[axis, q - 1], device_id=where(q), device_id_type=MESH)
            copy.start()
            copies.append(copy)
        for copy in copies:
            copy.wait()
        for q in range(7):
            message = message + buf[q]
    sums = jnp.sum(message, axis=1, keepdims=True)
    images = count * 2 * LANES
    scale = lax.rsqrt(sums[0:1] / images + mean_eps)
    for step in range(1, ITERS):
        scale = scale * lax.rsqrt(scale * scale * sums[step:step + 1] / images + mean_eps)
    vec_ref[...] = packed * scale


def power_call(part, vwin, idx, bins, deg, count):
    groups = idx.shape[0] // 8
    vmem = pl.BlockSpec(memory_space=pltpu.VMEM)
    n = len(STEPS)
    dma = pltpu.SemaphoreType.DMA
    return pl.pallas_call(
        lambda *refs: power_kernel(count, groups, *refs),
        out_shape=(jax.ShapeDtypeStruct(idx.shape, jnp.float32), jax.ShapeDtypeStruct((8, LANES), jnp.float32)),
        in_specs=[vmem] * 5,
        out_specs=(vmem, vmem),
        scratch_shapes=[pltpu.VMEM((7, PIECE, LANES), jnp.float32), pltpu.VMEM((8, PIECE, LANES), jnp.float32),
                        pltpu.VMEM((BLOCKS, 8, LANES), jnp.float32), pltpu.VMEM((BLOCKS, 8, LANES), jnp.float32),
                        pltpu.VMEM((8, 8, LANES), jnp.float32), pltpu.VMEM((8, 8, LANES), jnp.float32),
                        dma((7,)), dma((7,)), dma((7,)), dma((7,)), dma((2, n)), dma((2, n)), dma((2, 7)), dma((2, 7))],
        compiler_params=pltpu.CompilerParams(collective_id=1, has_side_effects=True),
        name="power",
    )(part, vwin, idx, bins, deg)


def shards(coef, neighbours, rot_bin, degree, v_init):
    rows = coef.shape[0]
    slots = neighbours.shape[0]
    count = lax.axis_size("img")
    offset = (neighbours // rows - lax.axis_index("img") + SPAN + count) % count
    position = offset * rows + neighbours % rows
    tall = lambda value: jnp.pad(value.reshape(2 * slots, LANES), ((0, SQ_ROW - 2 * slots), (0, 0)))
    idx = tall(position)
    bins = tall(rot_bin)
    deg = jnp.tile(degree.reshape(2, LANES), (4, 1))
    vec = jnp.tile(v_init.reshape(4, LANES), (2, 1))
    window, vwin = window_call(coef, vec, count)
    part = pair_call(idx, window, bins, slots)
    weights, vector = power_call(part.reshape(8, PIECE, LANES), vwin, idx, bins, deg, count)
    return vector[:4].reshape(2, rows), weights[:2 * slots].reshape(slots, rows)


def solution(mesh):
    return jax.shard_map(
        shards,
        mesh=mesh,
        in_specs=(P("img", "freq"), P(None, "img"), P(None, "img"), P("img"), P(None, "img")),
        out_specs=(P(None, "img"), P(None, "img")),
        check_vma=False,
    )
```

time: 1120 us -> 116 us (0.10)
  the two profiles are of different devices: /device:TPU:2 before, /device:TPU:8 now
where the time goes in v1:
time: 116 us; the launch traced here: 115 us
  Pallas kernels  107 us (92%)
  local copies, waits for them, and re-layouts  6.68 us (6%)
    pallas_call x1, Pallas kernels, power_call(): pl.pallas_call(lambda *refs: power_kernel(count, groups, *refs), out_shap...  45.8 us
    pallas_call x1, Pallas kernels, window_call(): pl.pallas_call(lambda *refs: window_kernel(count, *refs), out_shape=(jax....  41.5 us
    pallas_call x1, Pallas kernels, pair_call(): pl.pallas_call(lambda *refs: pair_kernel(slots, *refs), out_shape=jax.Sha...  19.8 us

profile of v1, /device:TPU:8, one launch (start us, length us, event | category | flops | bytes accessed | tf_op | source)
XLA Modules:
  0.0 115.3 jit_solution(6437493534424192103)
XLA Ops:
  0.6 0.0 copy-start
  0.6 0.7 tile.20
  1.3 0.6 tile.21
  1.9 41.5 %window.1 = (bf16[17,256,128]{2,1,0:T(8,128)(2,1)}, f32[17,8,128]{2,1,0:T(8,128)}) custom-call(bf16[256,128]{1,0:T(8,128)(2,1)} %refs_0_.1, f32[8,128]{1,0:T(8,128)} %bitcast.8), custom_call_target="tpu_custom_call" | custom-call | tf_op jit(solution)/shard_map/window/pallas_call | solution.py:79
  43.5 0.9 fusion.4
  44.4 0.6 pad.7.refs_0_.refs_2_
  45.0 0.8 reshape.28
  45.8 0.6 pad.8.refs_2_.refs_3_
  46.5 19.8 %pairs.1 = f32[192,128]{1,0:T(8,128)} custom-call(s32[104,128]{1,0:T(8,128)} %pad.7.refs_0_.refs_2_, bf16[17,256,128]{2,1,0:T(8,128)(2,1)} %get-tuple-element.6.refs_1_, s32[104,128]{1,0:T(8,128)} %pad.8.refs_2_.refs_3_), custom_call_target="tpu_custom_call" | custom-call | tf_op jit(solution)/shard_map/pairs/pallas_call | solution.py:152
  66.2 0.0 copy-done
  66.2 0.6 tile.24
  66.8 45.8 %power.1 = (f32[104,128]{1,0:T(8,128)}, f32[8,128]{1,0:T(8,128)}) custom-call(f32[8,24,128]{2,1,0:T(8,128)} %bitcast.5, f32[17,8,128]{2,1,0:T(8,128)} %get-tuple-element.7.refs_1_, s32[104,128]{1,0:T(8,128)} %pad.7.refs_0_.refs_2_, s32[104,128]{1,0:T(8,128)} %pad.8.refs_2_.refs_3_, s32[8,128]{1,0:T(8,128)} %bitcast.7), custom_call_target="tpu_custom_call" | custom-call | tf_op jit(solution)/shard_map/power/pallas_call | solution.py:306
  112.6 1.4 %reshape.31 = f32[50,256]{1,0:T(8,128)} reshape(f32[100,128]{1,0:T(8,128)} %bitcast.6) | data formatting | bytes 102400 | tf_op jit(solution)/shard_map/reshape | solution.py:334
  114.1 0.7 slice.6
  114.7 0.6 reshape.30
  (1 shorter events, 0.0 us)
Async XLA Ops:
  0.6 65.6 %copy-start = (s32[256]{0:T(256)S(1)}, s32[256]{0:T(256)}, u32[]{:S(2)}) copy-start(s32[256]{0:T(256)} %param.8) | copy-start | bytes 3076

commit v2 on v1

--- a/solution.py
+++ b/solution.py
@@ -15,6 +15,7 @@
 BLOCKS = 2 * SPAN + 1
 PIECE = 24
 SQ_ROW = 104
+OWN_ROW = SQ_ROW + 2 * BLOCKS
 
 sharpness = 64.0
 norm_eps = 1e-05
@@ -51,41 +52,104 @@
     pl.semaphore_wait(barrier, len(targets))
 
 
-def window_kernel(count, coef_ref, vec_ref, win_ref, vwin_ref, send, recv, vsend, vrecv, local):
+def ring(me, mine_z, mine_y):
+    y_at = lambda q: {"img": mine_z * 8 + lax.rem(mine_y + q, 8)}
+    z_at = lambda q: {"img": lax.rem(mine_z + q, 8) * 8 + mine_y}
+    return y_at, z_at
+
+
+def landing_slot(mine_y, hop):
+    if hop == -SPAN:
+        return 2 * SPAN
+    row = lax.div(mine_y + (hop + SPAN), SPAN) - 1
+    return mine_y + SPAN * row * row
+
+
+def window_kernel(count, coef_ref, nei_ref, bin_ref, v_ref, win_ref, vwin_ref, idx_ref, bins_ref, message,
+                  y_send, y_recv, z_send, z_recv, v_send, v_recv, local):
     me = lax.axis_index("img")
+    y, z = lax.rem(me, 8), lax.div(me, 8)
+    y_at, z_at = ring(me, z, y)
+    message[...] = jnp.zeros_like(message)
+    for part in range(2):
+        for half in range(2):
+            message[part * 2 + half:part * 2 + half + 1, :] = v_ref[part:part + 1, half * LANES:(half + 1) * LANES]
     greet([img_at(me, step, count) for step in STEPS])
-    copies = []
-    for n, step in enumerate(STEPS):
-        slot = SPAN - step
-        for src, dst, ss, rs in ((coef_ref, win_ref, send, recv), (vec_ref, vwin_ref, vsend, vrecv)):
-            copy = pltpu.make_async_remote_copy(
-                src_ref=src, dst_ref=dst.at[slot], send_sem=ss.at[n], recv_sem=rs.at[n],
-                device_id=img_at(me, step, count), device_id_type=MESH)
-            copy.start()
-            copies.append(copy)
-    own = pltpu.make_async_copy(coef_ref, win_ref.at[SPAN], local.at[0])
-    own_vec = pltpu.make_async_copy(vec_ref, vwin_ref.at[SPAN], local.at[1])
+    started = []
+
+    def send(src, dst, ss, rs, target):
+        copy = pltpu.make_async_remote_copy(
+            src_ref=src, dst_ref=dst, send_sem=ss, recv_sem=rs, device_id=target, device_id_type=MESH)
+        copy.start()
+        return copy
+
+    ways = (1, 7)
+    flows = [[send(coef_ref, win_ref.at[y], y_send.at[w, 0], y_recv.at[w, 0], y_at(ways[w]))] for w in range(2)]
+    rows = [send(coef_ref, win_ref.at[8 + y], z_send.at[7], z_recv.at[7], z_at(1)),
+            send(coef_ref, win_ref.at[16], z_send.at[8], z_recv.at[8], z_at(7))]
+    own = pltpu.make_async_copy(coef_ref, win_ref.at[y], local.at[0])
     own.start()
-    own_vec.start()
+    small = [send(message, vwin_ref.at[landing_slot(y, step)], v_send.at[n], v_recv.at[n], img_at(me, step, count))
+             for n, step in enumerate(STEPS)]
+    vwin_ref[y] = message[...]
+
+    slots = nei_ref.shape[0]
+    nei = nei_ref[...]
+    block = nei >> 8
+    hop = ((block - me + (SPAN + count)) & (count - 1)) - SPAN
+    slot = jnp.where(hop == SPAN, 2 * SPAN, (block & 7) + jnp.where((block >> 3) != z, SPAN, 0))
+    place = slot * (2 * LANES) + (nei & (2 * LANES - 1))
+    for half in range(2):
+        idx_ref[pl.ds(half, slots, stride=2), :] = place[:, half * LANES:(half + 1) * LANES]
+        bins_ref[pl.ds(half, slots, stride=2), :] = bin_ref[:, half * LANES:(half + 1) * LANES]
+    idx_ref[2 * slots:, :] = jnp.zeros((SQ_ROW - 2 * slots, LANES), jnp.int32)
+    bins_ref[2 * slots:, :] = jnp.zeros((SQ_ROW - 2 * slots, LANES), jnp.int32)
+
+    for q in range(1, 4):
+        for w in range(2):
+            from_block = lax.rem(y + (8 - q if w == 0 else q), 8)
+            turn = lax.div(y - q + 8, 8) if w == 0 else lax.div(y + q, 8)
+            flows[w][q - 1].wait_recv()
+            held = win_ref.at[from_block]
+            if q == 3:
+                span = pl.ds(w * LANES, LANES)
+                src = win_ref.at[from_block, span]
+            else:
+                src = held
+            flows[w].append(send(src, src, y_send.at[w, q], y_recv.at[w, q], y_at(ways[w])))
+            at = (q - 1) * 2 + w
+            rows.append(send(held, win_ref.at[8 + from_block], z_send.at[at], z_recv.at[at], z_at(1 + 6 * turn)))
+    for w in range(2):
+        flows[w][3].wait_recv()
+    far = lax.rem(y + 4, 8)
+    rows.append(send(win_ref.at[far], win_ref.at[8 + far], z_send.at[6], z_recv.at[6], z_at(1 + 6 * lax.div(y + 4, 8))))
+    for copy in rows:
+        copy.wait_recv()
+    for copy in rows + flows[0] + flows[1]:
+        copy.wait_send()
+    for copy in small:
+        copy.wait()
     own.wait()
-    own_vec.wait()
-    for copy in copies:
-        copy.wait()
-
-
-def window_call(coef, vec, count):
+
+
+def window_call(coef, neighbours, rot_bin, v_init, count):
     rows, width = coef.shape
     n = len(STEPS)
+    vmem = pl.BlockSpec(memory_space=pltpu.VMEM)
+    dma = pltpu.SemaphoreType.DMA
     return pl.pallas_call(
         lambda *refs: window_kernel(count, *refs),
         out_shape=(jax.ShapeDtypeStruct((BLOCKS, rows, width), coef.dtype),
-                   jax.ShapeDtypeStruct((BLOCKS, 8, LANES), jnp.float32)),
-        in_specs=[pl.BlockSpec(memory_space=pltpu.VMEM)] * 2,
-        out_specs=(pl.BlockSpec(memory_space=pltpu.VMEM),) * 2,
-        scratch_shapes=[pltpu.SemaphoreType.DMA((n,))] * 4 + [pltpu.SemaphoreType.DMA((2,))],
+                   jax.ShapeDtypeStruct((BLOCKS, 8, LANES), jnp.float32),
+                   jax.ShapeDtypeStruct((SQ_ROW, LANES), jnp.int32),
+                   jax.ShapeDtypeStruct((SQ_ROW, LANES), jnp.int32)),
+        in_specs=[vmem] * 4,
+        out_specs=(vmem,) * 4,
+        scratch_shapes=[pltpu.VMEM((8, LANES), jnp.float32), dma((2, 4)), dma((2, 4)), dma((9,)), dma((9,)),
+                        dma((n,)), dma((n,)), dma((1,))],
         compiler_params=pltpu.CompilerParams(collective_id=0, has_side_effects=True),
         name="window",
-    )(coef, vec)
+    )(coef, neighbours, rot_bin, v_init)
 
 
 def split_exact(value):
@@ -98,7 +162,7 @@
     return lax.dot_general(select, value, (((1,), (1,)), ((), ())), preferred_element_type=jnp.float32)
 
 
-def pair_kernel(slots, idx_ref, win_ref, bins_ref, out_ref, wide, turned, *tiles):
+def pair_kernel(slots, idx_ref, win_ref, bins_ref, out_ref, wide, own_tile, turned, *tiles):
     rows = win_ref.shape[1]
     first = lax.axis_index("freq") * (LANES // (2 * RADIAL))
     lane = lax.broadcasted_iota(jnp.int32, (8, 2 * LANES), 1)
@@ -116,7 +180,13 @@
             at = SQ_ROW + block * 2 + half
             out_ref[at:at + 1, :] = lane_sums(ones, split_exact(piece * piece))[0:1]
 
-    own = wide[SPAN * rows:(SPAN + 1) * rows, :]
+    slot = lax.rem(lax.axis_index("img"), 8)
+    own = win_ref[slot].astype(jnp.float32)
+    own_tile[...] = own
+    for half in range(rows // LANES):
+        piece = own[half * LANES:(half + 1) * LANES]
+        at = OWN_ROW + half
+        out_ref[at:at + 1, :] = lane_sums(ones, split_exact(piece * piece))[0:1]
     column = lax.broadcasted_iota(jnp.int32, own.shape, 1)
     turned[...] = jnp.where(column % (2 * RADIAL) < RADIAL,
                             pltpu.roll(own, LANES - RADIAL, 1), -pltpu.roll(own, RADIAL, 1))
@@ -133,8 +203,7 @@
             row = step * per + n
             half = n % 2
             other = tiles[n][...]
-            base = SPAN * rows + half * LANES
-            real = split_exact(wide[base:base + LANES, :] * other)
+            real = split_exact(own_tile[half * LANES:(half + 1) * LANES, :] * other)
             imag = split_exact(turned[half * LANES:(half + 1) * LANES, :] * other)
             sums = lane_sums(select, jnp.concatenate([real, imag], axis=0))
             units = bins_ref[pl.ds(row, 1), :].astype(jnp.float32) * freq
@@ -155,7 +224,7 @@
         in_specs=[pl.BlockSpec(memory_space=pltpu.SMEM), vmem, vmem],
         out_specs=vmem,
         scratch_shapes=[pltpu.VMEM((blocks * rows, width), jnp.float32),
-                        pltpu.VMEM((rows, width), jnp.float32)]
+                        pltpu.VMEM((rows, width), jnp.float32), pltpu.VMEM((rows, width), jnp.float32)]
         + [pltpu.VMEM((LANES, LANES), jnp.float32)] * 4,
         name="pairs",
     )(idx, window, bins)
@@ -182,14 +251,13 @@
 
 
 def power_kernel(count, groups, part_ref, vwin_ref, idx_ref, bins_ref, deg_ref, weights_ref, vec_ref,
-                 rs_buf, ag_buf, vec1, vec2, ynorm, znorm,
+                 wbuf, rs_buf, ag_buf, vec1, vec2, ynorm, znorm,
                  rs_send, rs_recv, ag_send, ag_recv, v_send, v_recv, n_send, n_recv):
     me = lax.axis_index("img")
     mine = lax.axis_index("freq")
-    y, z = lax.rem(me, 8), me // 8
+    y, z = lax.rem(me, 8), lax.div(me, 8)
     freq_at = lambda q: {"freq": lax.rem(mine + q, 8)}
-    y_at = lambda q: {"img": z * 8 + lax.rem(y + q, 8)}
-    z_at = lambda q: {"img": lax.rem(z + q, 8) * 8 + y}
+    y_at, z_at = ring(me, z, y)
     greet([img_at(me, step, count) for step in STEPS] + [freq_at(q) for q in range(1, 8)]
           + [y_at(q) for q in range(1, 8)] + [z_at(q) for q in range(1, 8)])
 
@@ -201,6 +269,7 @@
         copy.start()
         copies.append(copy)
     sub = lax.broadcasted_iota(jnp.int32, (8, LANES), 0)
+    degree = jnp.where(sub % 2 == 0, deg_ref[0:1, :], deg_ref[1:2, :])
     low, high, cosine, sine, valid = [], [], [], [], []
     for m in range(groups):
         idx = idx_ref[m * 8:(m + 1) * 8, :]
@@ -209,7 +278,7 @@
         cos, sin = cos_sin_turns(bins_ref[m * 8:(m + 1) * 8, :].astype(jnp.float32))
         cosine.append(cos)
         sine.append(sin)
-        valid.append((sub // 2 + m * 4) < deg_ref[...])
+        valid.append((sub // 2 + m * 4) < degree)
     for copy in copies:
         copy.wait()
     total = part_ref[mine]
@@ -231,7 +300,7 @@
         return ag_buf[piece, at:at + size, :]
 
     sq_row = lambda row: ag_row(SQ_ROW + row, 1)
-    own = jnp.where(sub % 2 == 0, sq_row(2 * SPAN), sq_row(2 * SPAN + 1))
+    own = jnp.where(sub % 2 == 0, ag_row(OWN_ROW, 1), ag_row(OWN_ROW + 1, 1))
     own_root = lax.rsqrt(own + norm_eps)
     (other_sq,) = pick(low, high, lambda row: (sq_row(row),))
     raw = []
@@ -244,9 +313,13 @@
     denom = fold(denom)
     for m in range(groups):
         weight = raw[m] / denom
-        weights_ref[m * 8:(m + 1) * 8, :] = weight
+        wbuf[m * 8:(m + 1) * 8, :] = weight
         cosine[m] = weight * cosine[m]
         sine[m] = weight * sine[m]
+
+    slots = weights_ref.shape[0]
+    for half in range(2):
+        weights_ref[:, half * LANES:(half + 1) * LANES] = wbuf[pl.ds(half, slots, stride=2), :]
 
     norms = []
     source = vwin_ref
@@ -264,11 +337,11 @@
         packed = jnp.where(sub % 4 < 2, real, imag)
         if step < ITERS - 1:
             into = (vec1, vec2)[step]
-            into[SPAN] = packed
+            into[y] = packed
             copies = []
             for n, hop in enumerate(STEPS):
                 copy = pltpu.make_async_remote_copy(
-                    src_ref=into.at[SPAN], dst_ref=into.at[SPAN - hop], send_sem=v_send.at[step, n],
+                    src_ref=into.at[y], dst_ref=into.at[landing_slot(y, hop)], send_sem=v_send.at[step, n],
                     recv_sem=v_recv.at[step, n], device_id=img_at(me, hop, count), device_id_type=MESH)
                 copy.start()
                 copies.append(copy)
@@ -295,20 +368,24 @@
     scale = lax.rsqrt(sums[0:1] / images + mean_eps)
     for step in range(1, ITERS):
         scale = scale * lax.rsqrt(scale * scale * sums[step:step + 1] / images + mean_eps)
-    vec_ref[...] = packed * scale
-
-
-def power_call(part, vwin, idx, bins, deg, count):
+    vector = packed * scale
+    for part in range(2):
+        for half in range(2):
+            row = part * 2 + half
+            vec_ref[part:part + 1, half * LANES:(half + 1) * LANES] = vector[row:row + 1, :]
+
+
+def power_call(part, vwin, idx, bins, deg, count, slots):
     groups = idx.shape[0] // 8
     vmem = pl.BlockSpec(memory_space=pltpu.VMEM)
     n = len(STEPS)
     dma = pltpu.SemaphoreType.DMA
     return pl.pallas_call(
         lambda *refs: power_kernel(count, groups, *refs),
-        out_shape=(jax.ShapeDtypeStruct(idx.shape, jnp.float32), jax.ShapeDtypeStruct((8, LANES), jnp.float32)),
+        out_shape=(jax.ShapeDtypeStruct((slots, 2 * LANES), jnp.float32), jax.ShapeDtypeStruct((2, 2 * LANES), jnp.float32)),
         in_specs=[vmem] * 5,
         out_specs=(vmem, vmem),
-        scratch_shapes=[pltpu.VMEM((7, PIECE, LANES), jnp.float32), pltpu.VMEM((8, PIECE, LANES), jnp.float32),
+        scratch_shapes=[pltpu.VMEM(idx.shape, jnp.float32), pltpu.VMEM((7, PIECE, LANES), jnp.float32), pltpu.VMEM((8, PIECE, LANES), jnp.float32),
                         pltpu.VMEM((BLOCKS, 8, LANES), jnp.float32), pltpu.VMEM((BLOCKS, 8, LANES), jnp.float32),
                         pltpu.VMEM((8, 8, LANES), jnp.float32), pltpu.VMEM((8, 8, LANES), jnp.float32),
                         dma((7,)), dma((7,)), dma((7,)), dma((7,)), dma((2, n)), dma((2, n)), dma((2, 7)), dma((2, 7))],
@@ -318,20 +395,13 @@
 
 
 def shards(coef, neighbours, rot_bin, degree, v_init):
-    rows = coef.shape[0]
     slots = neighbours.shape[0]
     count = lax.axis_size("img")
-    offset = (neighbours // rows - lax.axis_index("img") + SPAN + count) % count
-    position = offset * rows + neighbours % rows
-    tall = lambda value: jnp.pad(value.reshape(2 * slots, LANES), ((0, SQ_ROW - 2 * slots), (0, 0)))
-    idx = tall(position)
-    bins = tall(rot_bin)
-    deg = jnp.tile(degree.reshape(2, LANES), (4, 1))
-    vec = jnp.tile(v_init.reshape(4, LANES), (2, 1))
-    window, vwin = window_call(coef, vec, count)
+    window, vwin, idx, bins = window_call(coef, neighbours, rot_bin, v_init, count)
     part = pair_call(idx, window, bins, slots)
-    weights, vector = power_call(part.reshape(8, PIECE, LANES), vwin, idx, bins, deg, count)
-    return vector[:4].reshape(2, rows), weights[:2 * slots].reshape(slots, rows)
+    weights, vector = power_call(
+        part.reshape(8, PIECE, LANES), vwin, idx, bins, degree.reshape(2, LANES), count, slots)
+    return vector, weights
 
 
 def solution(mesh):

time: 116 us -> 102 us (0.88)
  Pallas kernels: 107 us -> 98.7 us
  local copies, waits for them, and re-layouts: 6.68 us -> 2.71 us
    pallas_call x1, Pallas kernels: 41.5 us -> 33.3 us  [window_call(): pl.pallas_call(lambda *refs: window_kernel(count, *refs), out_shape=(jax....]
    reshape x4 -> x0, local copies, waits for them, and re-layouts: 2.87 us -> none  [the longest x1 1.45 us: shards(): weights[:2 * slots].reshape(slots, rows)]
    unnamed x2, local copies, waits for them, and re-layouts: 0.01 us -> 2.71 us
    another operation x3 -> x0, local copies, waits for them, and re-layouts: 1.89 us -> none  [the longest x2 1.3 us: shards(): vec = jnp.tile(v_init.reshape(4, LANES), (2, 1))]
    pad x2 -> x0, local copies, waits for them, and re-layouts: 1.25 us -> none  [shards(): jnp.pad(value.reshape(2 * slots, LANES), ((0, SQ_ROW - 2 * slots), (0, 0)))]
where the time goes in v2:
time: 102 us
  Pallas kernels  98.7 us (97%)
  local copies, waits for them, and re-layouts  2.71 us (3%)
    pallas_call x1, Pallas kernels, power_call(): pl.pallas_call(lambda *refs: power_kernel(count, groups, *refs), out_shap...  45.5 us
    pallas_call x1, Pallas kernels, window_call(): pl.pallas_call(lambda *refs: window_kernel(count, *refs), out_shape=(jax....  33.3 us
    pallas_call x1, Pallas kernels, pair_call(): pl.pallas_call(lambda *refs: pair_kernel(slots, *refs), out_shape=jax.Sha...  19.9 us
    unnamed x2, local copies, waits for them, and re-layouts  2.71 us

profile of v2, /device:TPU:8, one launch (start us, length us, event | category | flops | bytes accessed | tf_op | source)
XLA Modules:
  0.0 102.1 jit_solution(971179809808839274)
XLA Ops:
  0.6 33.3 %window.1 = (bf16[17,256,128]{2,1,0:T(8,128)(2,1)}, f32[17,8,128]{2,1,0:T(8,128)}, s32[104,128]{1,0:T(8,128)}, s32[104,128]{1,0:T(8,128)}) custom-call(bf16[256,128]{1,0:T(8,128)(2,1)} %refs_0_.1, s32[50,256]{1,0:T(8,128)} %refs_1_.1, s32[50,256]{1,0:T(8,128)} %refs_2_.1, f32[2,256]{1,0:T(2,128)} %refs_3_.1), custom_call_target="tpu_custom_call" | custom-call | tf_op jit(solution)/shard_map/window/pallas_call | solution.py:140
  34.0 19.9 %pairs.1 = f32[192,128]{1,0:T(8,128)} custom-call(s32[104,128]{1,0:T(8,128)} %get-tuple-element.8.refs_0_.refs_2_, bf16[17,256,128]{2,1,0:T(8,128)(2,1)} %get-tuple-element.9.refs_1_, s32[104,128]{1,0:T(8,128)} %get-tuple-element.10.refs_2_.refs_3_), custom_call_target="tpu_custom_call" | custom-call | tf_op jit(solution)/shard_map/pairs/pallas_call | solution.py:221
  53.8 45.5 %power.1 = (f32[50,256]{1,0:T(8,128)}, f32[2,256]{1,0:T(2,128)}) custom-call(f32[8,24,128]{2,1,0:T(8,128)} %bitcast.2, f32[17,8,128]{2,1,0:T(8,128)} %get-tuple-element.11.refs_1_, s32[104,128]{1,0:T(8,128)} %get-tuple-element.8.refs_0_.refs_2_, s32[104,128]{1,0:T(8,128)} %get-tuple-element.10.refs_2_.refs_3_, s32[2,128]{1,0:T(2,128)} %bitcast.3), custom_call_target="tpu_custom_call" | custom-call | tf_op jit(solution)/shard_map/power/pallas_call | solution.py:383
  99.3 1.3 %copy.9 = f32[2,256]{1,0:T(2,128)} copy(f32[2,256]{1,0:T(2,128)} %get-tuple-element.16) | data formatting | bytes 4096
  100.6 1.4 %copy.10 = f32[50,256]{1,0:T(8,128)} copy(f32[50,256]{1,0:T(8,128)} %get-tuple-element.17) | data formatting | bytes 102400

commit v3 on v2

v3 whole, which is shorter than its diff:
```python
import math

import jax
import jax.numpy as jnp
from jax import lax
from jax.experimental import pallas as pl
from jax.experimental.pallas import tpu as pltpu
from jax.sharding import PartitionSpec as P

RADIAL = 8
BINS = 360
ITERS = 3
LANES = 128
SPAN = 8
BLOCKS = 2 * SPAN + 1
PIECE = 16
TALL = 104

sharpness = 64.0
norm_eps = 1e-05
mean_eps = 1e-06

MESH = pl.DeviceIdType.MESH
STEPS = [sign * dist for dist in range(SPAN, 0, -1) for sign in (1, -1)]


def cos_sin_turns(units):
    turns = jnp.floor((units + 0.5) * (1.0 / BINS))
    rest = units - turns * BINS
    quarter = jnp.floor((rest + 45.0) * (1.0 / 90.0) + 1e-3)
    x = (rest - quarter * 90.0) * (math.pi / 180.0)
    y = x * x
    s = x * (1.0 + y * (-1.0 / 6 + y * (1.0 / 120 + y * (-1.0 / 5040 + y * (1.0 / 362880)))))
    c = 1.0 + y * (-0.5 + y * (1.0 / 24 + y * (-1.0 / 720 + y * (1.0 / 40320))))
    odd = (quarter == 1.0) | (quarter == 3.0)
    cos = jnp.where(odd, s, c)
    sin = jnp.where(odd, c, s)
    cos = jnp.where((quarter == 1.0) | (quarter == 2.0), -cos, cos)
    sin = jnp.where((quarter == 2.0) | (quarter == 3.0), -sin, sin)
    return cos, sin


def img_at(me, step, count):
    return {"img": lax.rem(me + (step + count), count)}


def greet(targets):
    barrier = pltpu.get_barrier_semaphore()
    for target in targets:
        pl.semaphore_signal(barrier, inc=1, device_id=target, device_id_type=MESH)
    return lambda: pl.semaphore_wait(barrier, len(targets))


def ring(me, mine_z, mine_y):
    y_at = lambda q: {"img": mine_z * 8 + lax.rem(mine_y + q, 8)}
    z_at = lambda q: {"img": lax.rem(mine_z + q, 8) * 8 + mine_y}
    return y_at, z_at


def landing_slot(mine_y, hop):
    if hop == -SPAN:
        return 2 * SPAN
    row = lax.div(mine_y + (hop + SPAN), SPAN) - 1
    return mine_y + SPAN * row * row


def window_kernel(count, coef_ref, nei_ref, bin_ref, v_ref, win_ref, vwin_ref, idx_ref, bins_ref, message, squares,
                  y_send, y_recv, z_send, z_recv, v_send, v_recv, s_send, s_recv, local):
    me = lax.axis_index("img")
    mine = lax.axis_index("freq")
    y, z = lax.rem(me, 8), lax.div(me, 8)
    y_at, z_at = ring(me, z, y)
    freq_at = lambda q: {"freq": lax.rem(mine + q, 8)}
    met = greet([img_at(me, step, count) for step in STEPS] + [freq_at(q) for q in range(1, 8)])
    own = pltpu.make_async_copy(coef_ref, win_ref.at[y], local.at[0])
    own.start()
    ones = jnp.ones((8, 2 * LANES), jnp.bfloat16)
    for half in range(2):
        piece = coef_ref[half * LANES:(half + 1) * LANES, :].astype(jnp.float32)
        sums = lane_sums(ones, split_exact(piece * piece))
        if half == 0:
            first_sums = sums
    sub = lax.broadcasted_iota(jnp.int32, (8, LANES), 0)
    squares[mine] = jnp.where(sub % 2 == 0, first_sums, sums)
    met()

    def send(src, dst, ss, rs, target):
        copy = pltpu.make_async_remote_copy(
            src_ref=src, dst_ref=dst, send_sem=ss, recv_sem=rs, device_id=target, device_id_type=MESH)
        copy.start()
        return copy

    ways = (1, 7)
    chunk = lambda c: pl.ds(c * LANES, LANES)
    flows, rows = {}, []
    for c in range(2):
        for w in range(2):
            flows[w, 0, c] = send(coef_ref.at[chunk(c)], win_ref.at[y, chunk(c)], y_send.at[w, 0, c],
                                  y_recv.at[w, 0, c], y_at(ways[w]))
    for c in range(2):
        rows.append(send(coef_ref.at[chunk(c)], win_ref.at[8 + y, chunk(c)], z_send.at[7, c], z_recv.at[7, c], z_at(1)))
        rows.append(send(coef_ref.at[chunk(c)], win_ref.at[16, chunk(c)], z_send.at[8, c], z_recv.at[8, c], z_at(7)))
    sums = [send(squares.at[mine], squares.at[mine], s_send.at[q - 1], s_recv.at[q - 1], freq_at(q))
            for q in range(1, 8)]

    slots = nei_ref.shape[0]
    nei = nei_ref[...]
    block = nei >> 8
    hop = ((block - me + (SPAN + count)) & (count - 1)) - SPAN
    slot = jnp.where(hop == SPAN, 2 * SPAN, (block & 7) + jnp.where((block >> 3) != z, SPAN, 0))
    place = slot * (2 * LANES) + (nei & (2 * LANES - 1))
    for half in range(2):
        idx_ref[pl.ds(half, slots, stride=2), :] = place[:, half * LANES:(half + 1) * LANES]
        bins_ref[pl.ds(half, slots, stride=2), :] = bin_ref[:, half * LANES:(half + 1) * LANES]
    idx_ref[2 * slots:, :] = jnp.zeros((TALL - 2 * slots, LANES), jnp.int32)
    bins_ref[2 * slots:, :] = jnp.zeros((TALL - 2 * slots, LANES), jnp.int32)

    small = []
    for q in range(1, 5):
        for c in range(2):
            for w in range(2):
                if q == 4 and w != c:
                    continue
                block_at = lax.rem(y + (8 - q if w == 0 else q), 8)
                turn = lax.div(y - q + 8, 8) if w == 0 else lax.div(y + q, 8)
                if q == 4:
                    turn = lax.div(y + 4, 8)
                flows[w, q - 1, c].wait_recv()
                held = win_ref.at[block_at, chunk(c)]
                if q < 3 or (q == 3 and w == c):
                    flows[w, q, c] = send(held, held, y_send.at[w, q, c], y_recv.at[w, q, c], y_at(ways[w]))
                at = (q - 1) * 2 + w if q < 4 else 6
                rows.append(send(held, win_ref.at[8 + block_at, chunk(c)], z_send.at[at, c], z_recv.at[at, c],
                                 z_at(1 + 6 * turn)))
        if q == 1:
            for copy in sums:
                copy.wait()
            total = squares[0]
            for other in range(1, 8):
                total = total + squares[other]
            packed = total
            for part in range(2):
                for half in range(2):
                    value = v_ref[part:part + 1, half * LANES:(half + 1) * LANES]
                    packed = jnp.where(sub == part * 2 + half, value, packed)
            message[...] = packed
            vwin_ref[y] = packed
            small = [send(message, vwin_ref.at[landing_slot(y, step)], v_send.at[n], v_recv.at[n],
                          img_at(me, step, count)) for n, step in enumerate(STEPS)]
    for copy in small + rows:
        copy.wait()
    for copy in flows.values():
        copy.wait_send()
    own.wait()


def window_call(coef, neighbours, rot_bin, v_init, count):
    rows, width = coef.shape
    n = len(STEPS)
    vmem = pl.BlockSpec(memory_space=pltpu.VMEM)
    dma = pltpu.SemaphoreType.DMA
    return pl.pallas_call(
        lambda *refs: window_kernel(count, *refs),
        out_shape=(jax.ShapeDtypeStruct((BLOCKS, rows, width), coef.dtype),
                   jax.ShapeDtypeStruct((BLOCKS, 8, LANES), jnp.float32),
                   jax.ShapeDtypeStruct((TALL, LANES), jnp.int32),
                   jax.ShapeDtypeStruct((TALL, LANES), jnp.int32)),
        in_specs=[vmem] * 4,
        out_specs=(vmem,) * 4,
        scratch_shapes=[pltpu.VMEM((8, LANES), jnp.float32), pltpu.VMEM((8, 8, LANES), jnp.float32),
                        dma((2, 4, 2)), dma((2, 4, 2)), dma((9, 2)), dma((9, 2)),
                        dma((n,)), dma((n,)), dma((7,)), dma((7,)), dma((1,))],
        compiler_params=pltpu.CompilerParams(collective_id=0, has_side_effects=True),
        name="window",
    )(coef, neighbours, rot_bin, v_init)


def split_exact(value):
    high = value.astype(jnp.bfloat16)
    low = (value - high.astype(jnp.float32)).astype(jnp.bfloat16)
    return jnp.concatenate([high, low], axis=1)


def lane_sums(select, value):
    return lax.dot_general(select, value, (((1,), (1,)), ((), ())), preferred_element_type=jnp.float32)


def pair_kernel(slots, idx_ref, win_ref, bins_ref, out_ref, wide, own_tile, turned, *tiles):
    rows = win_ref.shape[1]
    first = lax.axis_index("freq") * (LANES // (2 * RADIAL))
    lane = lax.broadcasted_iota(jnp.int32, (8, 2 * LANES), 1)
    sub = lax.broadcasted_iota(jnp.int32, (8, 2 * LANES), 0)
    select = jnp.where((lane % LANES) // (2 * RADIAL) == sub, 1.0, 0.0).astype(jnp.bfloat16)
    freq = (first + lax.broadcasted_iota(jnp.int32, (8, LANES), 0)).astype(jnp.float32)
    out_ref[...] = jnp.zeros_like(out_ref)

    for block in range(BLOCKS):
        wide[block * rows:(block + 1) * rows, :] = win_ref[block].astype(jnp.float32)

    slot = lax.rem(lax.axis_index("img"), 8)
    own = win_ref[slot].astype(jnp.float32)
    own_tile[...] = own
    column = lax.broadcasted_iota(jnp.int32, own.shape, 1)
    turned[...] = jnp.where(column % (2 * RADIAL) < RADIAL,
                            pltpu.roll(own, LANES - RADIAL, 1), -pltpu.roll(own, RADIAL, 1))

    per = len(tiles)

    def body(step, carry):
        for n in range(per):
            row = step * per + n
            tile = tiles[n]
            for pair in range(LANES):
                tile[pair:pair + 1, :] = wide[pl.ds(idx_ref[row, pair], 1), :]
        for n in range(per):
            row = step * per + n
            half = n % 2
            other = tiles[n][...]
            real = split_exact(own_tile[half * LANES:(half + 1) * LANES, :] * other)
            imag = split_exact(turned[half * LANES:(half + 1) * LANES, :] * other)
            sums = lane_sums(select, jnp.concatenate([real, imag], axis=0))
            units = bins_ref[pl.ds(row, 1), :].astype(jnp.float32) * freq
            cos, sin = cos_sin_turns(units)
            terms = sums[:, :LANES] * cos - sums[:, LANES:] * sin
            out_ref[pl.ds(row, 1), :] = jnp.sum(terms, axis=0, keepdims=True)
        return carry

    lax.fori_loop(0, 2 * slots // per, body, 0)


def pair_call(idx, window, bins, slots):
    blocks, rows, width = window.shape
    vmem = pl.BlockSpec(memory_space=pltpu.VMEM)
    return pl.pallas_call(
        lambda *refs: pair_kernel(slots, *refs),
        out_shape=jax.ShapeDtypeStruct((8 * PIECE, LANES), jnp.float32),
        in_specs=[pl.BlockSpec(memory_space=pltpu.SMEM), vmem, vmem],
        out_specs=vmem,
        scratch_shapes=[pltpu.VMEM((blocks * rows, width), jnp.float32),
                        pltpu.VMEM((rows, width), jnp.float32), pltpu.VMEM((rows, width), jnp.float32)]
        + [pltpu.VMEM((LANES, LANES), jnp.float32)] * 4,
        name="pairs",
    )(idx, window, bins)


def pick(low, high, ref, lines):
    found = []
    for where, at in zip(low, high):
        got = [None] * len(lines)
        for row in range(BLOCKS * 2):
            hit = at == row
            for n, line in enumerate(lines):
                first = line + row % 2
                wide = jnp.broadcast_to(ref[row // 2, first:first + 1, :], (8, LANES))
                new = jnp.take_along_axis(wide, where, axis=1, mode="promise_in_bounds")
                got[n] = new if row == 0 else jnp.where(hit, new, got[n])
        found.append(got)
    return found


def fold(total):
    total = total + pltpu.roll(total, 4, 0)
    return total + pltpu.roll(total, 2, 0)


def power_kernel(count, groups, part_ref, vwin_ref, idx_ref, bins_ref, deg_ref, weights_ref, vec_ref,
                 cos_buf, sin_buf, real_buf, imag_buf, root_buf, rs_buf, ag_buf, vec1, vec2, ynorm, znorm,
                 rs_send, rs_recv, ag_send, ag_recv, v_send, v_recv, n_send, n_recv):
    me = lax.axis_index("img")
    mine = lax.axis_index("freq")
    y, z = lax.rem(me, 8), lax.div(me, 8)
    freq_at = lambda q: {"freq": lax.rem(mine + q, 8)}
    y_at, z_at = ring(me, z, y)
    met = greet([img_at(me, step, count) for step in STEPS] + [freq_at(q) for q in range(1, 8)]
                + [y_at(q) for q in range(1, 8)] + [z_at(q) for q in range(1, 8)])
    sub = lax.broadcasted_iota(jnp.int32, (8, LANES), 0)
    degree = jnp.where(sub % 2 == 0, deg_ref[0:1, :], deg_ref[1:2, :])
    low = [idx_ref[m * 8:(m + 1) * 8, :] & (LANES - 1) for m in range(groups)]
    high = [idx_ref[m * 8:(m + 1) * 8, :] >> 7 for m in range(groups)]
    own_sq = vwin_ref[y]
    own_root = lax.rsqrt(jnp.where(sub % 2 == 0, own_sq[4:5], own_sq[5:6]) + norm_eps)
    for m, (real, imag, square) in enumerate(pick(low, high, vwin_ref, (0, 2, 4))):
        cos, sin = cos_sin_turns(bins_ref[m * 8:(m + 1) * 8, :].astype(jnp.float32))
        cos_buf[m] = cos
        sin_buf[m] = sin
        real_buf[m] = cos * real - sin * imag
        imag_buf[m] = sin * real + cos * imag
        root_buf[m] = lax.rsqrt(square + norm_eps) * own_root
    met()

    copies = []
    for q in range(1, 8):
        copy = pltpu.make_async_remote_copy(
            src_ref=part_ref.at[lax.rem(mine + q, 8)], dst_ref=rs_buf.at[q - 1],
            send_sem=rs_send.at[q - 1], recv_sem=rs_recv.at[q - 1], device_id=freq_at(q), device_id_type=MESH)
        copy.start()
        copies.append(copy)
    for copy in copies:
        copy.wait()
    total = part_ref[mine]
    for q in range(7):
        total = total + rs_buf[q]
    ag_buf[mine] = total
    copies = []
    for q in range(1, 8):
        copy = pltpu.make_async_remote_copy(
            src_ref=ag_buf.at[mine], dst_ref=ag_buf.at[mine],
            send_sem=ag_send.at[q - 1], recv_sem=ag_recv.at[q - 1], device_id=freq_at(q), device_id_type=MESH)
        copy.start()
        copies.append(copy)
    for copy in copies:
        copy.wait()

    def ag_row(row, size):
        piece, at = row // PIECE, row % PIECE
        return ag_buf[piece, at:at + size, :]

    denom = jnp.zeros((8, LANES), jnp.float32)
    for m in range(groups):
        cos_sim = ag_row(m * 8, 8) * root_buf[m]
        raw = jnp.where((sub // 2 + m * 4) < degree, jnp.exp(sharpness * cos_sim), 0.0)
        weights_ref[m * 8:(m + 1) * 8, :] = raw
        denom = denom + raw
    share = 1.0 / fold(denom)
    for m in range(groups):
        weights_ref[m * 8:(m + 1) * 8, :] = weights_ref[m * 8:(m + 1) * 8, :] * share

    norms = []
    source = None
    for step in range(ITERS):
        real = imag = jnp.zeros((8, LANES), jnp.float32)
        picked = pick(low, high, source, (0, 2)) if step else [None] * groups
        for m, at in enumerate(picked):
            weight = weights_ref[m * 8:(m + 1) * 8, :]
            if step:
                real_at, imag_at = at
                real = real + weight * (cos_buf[m] * real_at - sin_buf[m] * imag_at)
                imag = imag + weight * (sin_buf[m] * real_at + cos_buf[m] * imag_at)
            else:
                real = real + weight * real_buf[m]
                imag = imag + weight * imag_buf[m]
        real, imag = fold(real), fold(imag)
        square = real * real + imag * imag
        norms.append(square + pltpu.roll(square, 1, 0))
        packed = jnp.where(sub % 4 < 2, real, imag)
        if step < ITERS - 1:
            into = (vec1, vec2)[step]
            into[y] = packed
            copies = []
            for n, hop in enumerate(STEPS):
                copy = pltpu.make_async_remote_copy(
                    src_ref=into.at[y], dst_ref=into.at[landing_slot(y, hop)], send_sem=v_send.at[step, n],
                    recv_sem=v_recv.at[step, n], device_id=img_at(me, hop, count), device_id_type=MESH)
                copy.start()
                copies.append(copy)
            for copy in copies:
                copy.wait()
            source = into

    message = jnp.where(sub == 0, norms[0], jnp.where(sub == 1, norms[1], norms[2]))
    for axis, (buf, where) in enumerate(((ynorm, y_at), (znorm, z_at))):
        buf[7] = message
        copies = []
        for q in range(1, 8):
            copy = pltpu.make_async_remote_copy(
                src_ref=buf.at[7], dst_ref=buf.at[q - 1], send_sem=n_send.at[axis, q - 1],
                recv_sem=n_recv.at[axis, q - 1], device_id=where(q), device_id_type=MESH)
            copy.start()
            copies.append(copy)
        for copy in copies:
            copy.wait()
        for q in range(7):
            message = message + buf[q]
    sums = jnp.sum(message, axis=1, keepdims=True)
    images = count * 2 * LANES
    scale = lax.rsqrt(sums[0:1] / images + mean_eps)
    for step in range(1, ITERS):
        scale = scale * lax.rsqrt(scale * scale * sums[step:step + 1] / images + mean_eps)
    vec_ref[...] = packed * scale


def finish_kernel(tall_ref, packed_ref, weights_ref, vec_ref):
    slots = weights_ref.shape[0]
    for half in range(2):
        lanes = slice(half * LANES, (half + 1) * LANES)
        weights_ref[:, lanes] = tall_ref[pl.ds(half, slots, stride=2), :]
        for part in range(2):
            vec_ref[part:part + 1, lanes] = packed_ref[part * 2 + half:part * 2 + half + 1, :]


def power_call(part, vwin, idx, bins, deg, count):
    groups = idx.shape[0] // 8
    vmem = pl.BlockSpec(memory_space=pltpu.VMEM)
    n = len(STEPS)
    dma = pltpu.SemaphoreType.DMA
    return pl.pallas_call(
        lambda *refs: power_kernel(count, groups, *refs),
        out_shape=(jax.ShapeDtypeStruct(idx.shape, jnp.float32), jax.ShapeDtypeStruct((8, LANES), jnp.float32)),
        in_specs=[vmem] * 5,
        out_specs=(vmem, vmem),
        scratch_shapes=[pltpu.VMEM((groups, 8, LANES), jnp.float32)] * 5 + [pltpu.VMEM((7, PIECE, LANES), jnp.float32), pltpu.VMEM((8, PIECE, LANES), jnp.float32),
                        pltpu.VMEM((BLOCKS, 8, LANES), jnp.float32), pltpu.VMEM((BLOCKS, 8, LANES), jnp.float32),
                        pltpu.VMEM((8, 8, LANES), jnp.float32), pltpu.VMEM((8, 8, LANES), jnp.float32),
                        dma((7,)), dma((7,)), dma((7,)), dma((7,)), dma((2, n)), dma((2, n)), dma((2, 7)), dma((2, 7))],
        compiler_params=pltpu.CompilerParams(collective_id=1, has_side_effects=True),
        name="power",
    )(part, vwin, idx, bins, deg)


def shards(coef, neighbours, rot_bin, degree, v_init):
    slots = neighbours.shape[0]
    count = lax.axis_size("img")
    window, vwin, idx, bins = window_call(coef, neighbours, rot_bin, v_init, count)
    part = pair_call(idx, window, bins, slots)
    tall, packed = power_call(part.reshape(8, PIECE, LANES), vwin, idx, bins, degree.reshape(2, LANES), count)
    vmem = pl.BlockSpec(memory_space=pltpu.VMEM)
    weights, vector = pl.pallas_call(
        finish_kernel,
        out_shape=(jax.ShapeDtypeStruct(neighbours.shape, jnp.float32), jax.ShapeDtypeStruct(v_init.shape, jnp.float32)),
        in_specs=[vmem] * 2,
        out_specs=(vmem, vmem),
        name="finish",
    )(tall, packed)
    return vector, weights


def solution(mesh):
    return jax.shard_map(
        shards,
        mesh=mesh,
        in_specs=(P("img", "freq"), P(None, "img"), P(None, "img"), P("img"), P(None, "img")),
        out_specs=(P(None, "img"), P(None, "img")),
        check_vma=False,
    )
```

time: 102 us -> 92.8 us (0.910)
  the two profiles are of different devices: /device:TPU:8 before, /device:TPU:2 now
where the time goes in v3:
time: 92.8 us; the launch traced here: 92.5 us
  Pallas kernels  91.9 us (99%)
    pallas_call x1, Pallas kernels, power_call(): pl.pallas_call(lambda *refs: power_kernel(count, groups, *refs), out_shap...  37.3 us
    pallas_call x1, Pallas kernels, window_call(): pl.pallas_call(lambda *refs: window_kernel(count, *refs), out_shape=(jax....  33.9 us
    pallas_call x1, Pallas kernels, pair_call(): pl.pallas_call(lambda *refs: pair_kernel(slots, *refs), out_shape=jax.Sha...  19.2 us

profile of v3, /device:TPU:2, one launch (start us, length us, event | category | flops | bytes accessed | tf_op | source)
XLA Modules:
  0.0 92.5 jit_solution(5997391072005898212)
XLA Ops:
  0.6 33.9 %window.1 = (bf16[17,256,128]{2,1,0:T(8,128)(2,1)}, f32[17,8,128]{2,1,0:T(8,128)}, s32[104,128]{1,0:T(8,128)}, s32[104,128]{1,0:T(8,128)}) custom-call(bf16[256,128]{1,0:T(8,128)(2,1)} %refs_0_.1, s32[50,256]{1,0:T(8,128)} %refs_1_.1, s32[50,256]{1,0:T(8,128)} %refs_2_.1, f32[2,256]{1,0:T(2,128)} %refs_3_.1), custom_call_target="tpu_custom_call" | custom-call | tf_op jit(solution)/shard_map/window/pallas_call | solution.py:162
  34.6 19.2 %pairs.1 = f32[128,128]{1,0:T(8,128)} custom-call(s32[104,128]{1,0:T(8,128)} %get-tuple-element.10.refs_0_.refs_2_, bf16[17,256,128]{2,1,0:T(8,128)(2,1)} %get-tuple-element.11.refs_1_, s32[104,128]{1,0:T(8,128)} %get-tuple-element.12.refs_2_.refs_3_), custom_call_target="tpu_custom_call" | custom-call | tf_op jit(solution)/shard_map/pairs/pallas_call | solution.py:234
  53.8 37.3 %power.1 = (f32[104,128]{1,0:T(8,128)}, f32[8,128]{1,0:T(8,128)}) custom-call(f32[8,16,128]{2,1,0:T(8,128)} %bitcast.2, f32[17,8,128]{2,1,0:T(8,128)} %get-tuple-element.13.refs_1_, s32[104,128]{1,0:T(8,128)} %get-tuple-element.10.refs_0_.refs_2_, s32[104,128]{1,0:T(8,128)} %get-tuple-element.12.refs_2_.refs_3_, s32[2,128]{1,0:T(2,128)} %bitcast.3), custom_call_target="tpu_custom_call" | custom-call | tf_op jit(solution)/shard_map/power/pallas_call | solution.py:396
  91.1 1.4 %finish.1 = (f32[50,256]{1,0:T(8,128)}, f32[2,256]{1,0:T(2,128)}) custom-call(f32[104,128]{1,0:T(8,128)} %get-tuple-element.14.tall_ref, f32[8,128]{1,0:T(8,128)} %get-tuple-element.15.packed_ref), custom_call_target="tpu_custom_call" | custom-call | tf_op jit(solution)/shard_map/finish/pallas_call | solution.py:417

commit v4 on v3

--- a/solution.py
+++ b/solution.py
@@ -185,60 +185,73 @@
     return lax.dot_general(select, value, (((1,), (1,)), ((), ())), preferred_element_type=jnp.float32)
 
 
-def pair_kernel(slots, idx_ref, win_ref, bins_ref, out_ref, wide, own_tile, turned, *tiles):
+def pair_kernel(groups, idx_ref, win_ref, bins_ref, out_ref, wide, own_tile, turned, places, arrived, *tiles):
     rows = win_ref.shape[1]
+    fetch = lambda group, at: pltpu.make_async_copy(idx_ref.at[group], places[at], arrived.at[at])
+    fetch(0, 0).start()
+    fetch(1, 1).start()
     first = lax.axis_index("freq") * (LANES // (2 * RADIAL))
     lane = lax.broadcasted_iota(jnp.int32, (8, 2 * LANES), 1)
     sub = lax.broadcasted_iota(jnp.int32, (8, 2 * LANES), 0)
     select = jnp.where((lane % LANES) // (2 * RADIAL) == sub, 1.0, 0.0).astype(jnp.bfloat16)
     freq = (first + lax.broadcasted_iota(jnp.int32, (8, LANES), 0)).astype(jnp.float32)
-    out_ref[...] = jnp.zeros_like(out_ref)
+    line = lax.broadcasted_iota(jnp.int32, (8, LANES), 0)
 
     for block in range(BLOCKS):
         wide[block * rows:(block + 1) * rows, :] = win_ref[block].astype(jnp.float32)
-
-    slot = lax.rem(lax.axis_index("img"), 8)
-    own = win_ref[slot].astype(jnp.float32)
+    own = win_ref[lax.rem(lax.axis_index("img"), 8)].astype(jnp.float32)
     own_tile[...] = own
     column = lax.broadcasted_iota(jnp.int32, own.shape, 1)
     turned[...] = jnp.where(column % (2 * RADIAL) < RADIAL,
                             pltpu.roll(own, LANES - RADIAL, 1), -pltpu.roll(own, RADIAL, 1))
-
-    per = len(tiles)
-
-    def body(step, carry):
-        for n in range(per):
-            row = step * per + n
-            tile = tiles[n]
+    for group in range(groups, 16):
+        out_ref[group] = jnp.zeros((8, LANES), jnp.float32)
+
+    def one_group(group, at, then=None):
+        fetch(group, at).wait()
+        place = places[at]
+        for n in range(8):
             for pair in range(LANES):
-                tile[pair:pair + 1, :] = wide[pl.ds(idx_ref[row, pair], 1), :]
-        for n in range(per):
-            row = step * per + n
-            half = n % 2
+                tiles[n][pair:pair + 1, :] = wide[pl.ds(place[n, pair], 1), :]
+        if then is not None:
+            fetch(then, at).start()
+        result = jnp.zeros((8, LANES), jnp.float32)
+        for n in range(8):
+            half = slice((n % 2) * LANES, (n % 2 + 1) * LANES)
             other = tiles[n][...]
-            real = split_exact(own_tile[half * LANES:(half + 1) * LANES, :] * other)
-            imag = split_exact(turned[half * LANES:(half + 1) * LANES, :] * other)
+            real = split_exact(own_tile[half, :] * other)
+            imag = split_exact(turned[half, :] * other)
             sums = lane_sums(select, jnp.concatenate([real, imag], axis=0))
-            units = bins_ref[pl.ds(row, 1), :].astype(jnp.float32) * freq
+            units = bins_ref[group, n:n + 1, :].astype(jnp.float32) * freq
             cos, sin = cos_sin_turns(units)
             terms = sums[:, :LANES] * cos - sums[:, LANES:] * sin
-            out_ref[pl.ds(row, 1), :] = jnp.sum(terms, axis=0, keepdims=True)
+            result = jnp.where(line == n, jnp.sum(terms, axis=0, keepdims=True), result)
+        out_ref[group] = result
+
+    def body(step, carry):
+        one_group(2 * step, 0, 2 * step + 2)
+        one_group(2 * step + 1, 1, jnp.minimum(2 * step + 3, groups - 1))
         return carry
 
-    lax.fori_loop(0, 2 * slots // per, body, 0)
-
-
-def pair_call(idx, window, bins, slots):
+    lax.fori_loop(0, groups // 2, body, 0)
+    one_group(groups - 1, 0)
+    fetch(groups - 1, 1).wait()
+
+
+def pair_call(idx, window, bins):
     blocks, rows, width = window.shape
+    groups = idx.shape[0]
     vmem = pl.BlockSpec(memory_space=pltpu.VMEM)
     return pl.pallas_call(
-        lambda *refs: pair_kernel(slots, *refs),
-        out_shape=jax.ShapeDtypeStruct((8 * PIECE, LANES), jnp.float32),
-        in_specs=[pl.BlockSpec(memory_space=pltpu.SMEM), vmem, vmem],
+        lambda *refs: pair_kernel(groups, *refs[:7], refs[7:9], *refs[9:]),
+        out_shape=jax.ShapeDtypeStruct((16, 8, LANES), jnp.float32),
+        in_specs=[pl.BlockSpec(memory_space=pl.ANY), vmem, vmem],
         out_specs=vmem,
         scratch_shapes=[pltpu.VMEM((blocks * rows, width), jnp.float32),
-                        pltpu.VMEM((rows, width), jnp.float32), pltpu.VMEM((rows, width), jnp.float32)]
-        + [pltpu.VMEM((LANES, LANES), jnp.float32)] * 4,
+                        pltpu.VMEM((rows, width), jnp.float32), pltpu.VMEM((rows, width), jnp.float32),
+                        pltpu.SMEM((8, LANES), jnp.int32), pltpu.SMEM((8, LANES), jnp.int32),
+                        pltpu.SemaphoreType.DMA((2,))]
+        + [pltpu.VMEM((LANES, LANES), jnp.float32)] * 8,
         name="pairs",
     )(idx, window, bins)
 
@@ -408,10 +421,10 @@
 
 
 def shards(coef, neighbours, rot_bin, degree, v_init):
-    slots = neighbours.shape[0]
     count = lax.axis_size("img")
     window, vwin, idx, bins = window_call(coef, neighbours, rot_bin, v_init, count)
-    part = pair_call(idx, window, bins, slots)
+    groups = lambda value: value.reshape(TALL // 8, 8, LANES)
+    part = pair_call(groups(idx), window, groups(bins))
     tall, packed = power_call(part.reshape(8, PIECE, LANES), vwin, idx, bins, degree.reshape(2, LANES), count)
     vmem = pl.BlockSpec(memory_space=pltpu.VMEM)
     weights, vector = pl.pallas_call(

time: 92.8 us -> 88.7 us (0.956)
  Pallas kernels: 91.9 us -> 87.7 us
    pallas_call x1, Pallas kernels: 19.2 us -> 15 us  [pair_call(): pl.pallas_call(lambda *refs: pair_kernel(groups, *refs[:7], refs[7:9], *r...]
where the time goes in v4:
time: 88.7 us; the launch traced here: 88.4 us
  Pallas kernels  87.7 us (99%)
    pallas_call x1, Pallas kernels, power_call(): pl.pallas_call(lambda *refs: power_kernel(count, groups, *refs), out_shap...  37.3 us
    pallas_call x1, Pallas kernels, window_call(): pl.pallas_call(lambda *refs: window_kernel(count, *refs), out_shape=(jax....  33.9 us
    pallas_call x1, Pallas kernels, pair_call(): pl.pallas_call(lambda *refs: pair_kernel(groups, *refs[:7], refs[7:9], *r...  15 us

profile of v4, /device:TPU:2, one launch (start us, length us, event | category | flops | bytes accessed | tf_op | source)
XLA Modules:
  0.0 88.4 jit_solution(9207821439387023742)
XLA Ops:
  0.6 33.9 %window.1 = (bf16[17,256,128]{2,1,0:T(8,128)(2,1)}, f32[17,8,128]{2,1,0:T(8,128)}, s32[104,128]{1,0:T(8,128)}, s32[104,128]{1,0:T(8,128)}) custom-call(bf16[256,128]{1,0:T(8,128)(2,1)} %refs_0_.1, s32[50,256]{1,0:T(8,128)} %refs_1_.1, s32[50,256]{1,0:T(8,128)} %refs_2_.1, f32[2,256]{1,0:T(2,128)} %refs_3_.1), custom_call_target="tpu_custom_call" | custom-call | tf_op jit(solution)/shard_map/window/pallas_call | solution.py:162
  34.6 15.0 %pairs.1 = f32[16,8,128]{2,1,0:T(8,128)} custom-call(s32[13,8,128]{2,1,0:T(8,128)} %bitcast.5, bf16[17,256,128]{2,1,0:T(8,128)(2,1)} %get-tuple-element.11.refs_1_, s32[13,8,128]{2,1,0:T(8,128)} %bitcast.6), custom_call_target="tpu_custom_call" | custom-call | tf_op jit(solution)/shard_map/pairs/pallas_call | solution.py:245
  49.6 37.3 %power.1 = (f32[104,128]{1,0:T(8,128)}, f32[8,128]{1,0:T(8,128)}) custom-call(f32[8,16,128]{2,1,0:T(8,128)} %bitcast.4, f32[17,8,128]{2,1,0:T(8,128)} %get-tuple-element.13.refs_1_, s32[104,128]{1,0:T(8,128)} %get-tuple-element.10.refs_2_, s32[104,128]{1,0:T(8,128)} %get-tuple-element.12.refs_3_, s32[2,128]{1,0:T(2,128)} %bitcast.7), custom_call_target="tpu_custom_call" | custom-call | tf_op jit(solution)/shard_map/power/pallas_call | solution.py:409
  87.0 1.4 %finish.1 = (f32[50,256]{1,0:T(8,128)}, f32[2,256]{1,0:T(2,128)}) custom-call(f32[104,128]{1,0:T(8,128)} %get-tuple-element.14.tall_ref, f32[8,128]{1,0:T(8,128)} %get-tuple-element.15.packed_ref), custom_call_target="tpu_custom_call" | custom-call | tf_op jit(solution)/shard_map/finish/pallas_call | solution.py:430

commit v5 on v4

--- a/solution.py
+++ b/solution.py
@@ -13,7 +13,6 @@
 LANES = 128
 SPAN = 8
 BLOCKS = 2 * SPAN + 1
-PIECE = 16
 TALL = 104
 
 sharpness = 64.0
@@ -64,14 +63,13 @@
     return mine_y + SPAN * row * row
 
 
-def window_kernel(count, coef_ref, nei_ref, bin_ref, v_ref, win_ref, vwin_ref, idx_ref, bins_ref, message, squares,
-                  y_send, y_recv, z_send, z_recv, v_send, v_recv, s_send, s_recv, local):
+def window_part(count, met, coef_ref, nei_ref, bin_ref, v_ref, win_ref, vwin_ref, idx_ref, bins_ref, message, squares,
+                y_send, y_recv, z_send, z_recv, v_send, v_recv, s_send, s_recv, local):
     me = lax.axis_index("img")
     mine = lax.axis_index("freq")
     y, z = lax.rem(me, 8), lax.div(me, 8)
     y_at, z_at = ring(me, z, y)
     freq_at = lambda q: {"freq": lax.rem(mine + q, 8)}
-    met = greet([img_at(me, step, count) for step in STEPS] + [freq_at(q) for q in range(1, 8)])
     own = pltpu.make_async_copy(coef_ref, win_ref.at[y], local.at[0])
     own.start()
     ones = jnp.ones((8, 2 * LANES), jnp.bfloat16)
@@ -154,27 +152,6 @@
     own.wait()
 
 
-def window_call(coef, neighbours, rot_bin, v_init, count):
-    rows, width = coef.shape
-    n = len(STEPS)
-    vmem = pl.BlockSpec(memory_space=pltpu.VMEM)
-    dma = pltpu.SemaphoreType.DMA
-    return pl.pallas_call(
-        lambda *refs: window_kernel(count, *refs),
-        out_shape=(jax.ShapeDtypeStruct((BLOCKS, rows, width), coef.dtype),
-                   jax.ShapeDtypeStruct((BLOCKS, 8, LANES), jnp.float32),
-                   jax.ShapeDtypeStruct((TALL, LANES), jnp.int32),
-                   jax.ShapeDtypeStruct((TALL, LANES), jnp.int32)),
-        in_specs=[vmem] * 4,
-        out_specs=(vmem,) * 4,
-        scratch_shapes=[pltpu.VMEM((8, LANES), jnp.float32), pltpu.VMEM((8, 8, LANES), jnp.float32),
-                        dma((2, 4, 2)), dma((2, 4, 2)), dma((9, 2)), dma((9, 2)),
-                        dma((n,)), dma((n,)), dma((7,)), dma((7,)), dma((1,))],
-        compiler_params=pltpu.CompilerParams(collective_id=0, has_side_effects=True),
-        name="window",
-    )(coef, neighbours, rot_bin, v_init)
-
-
 def split_exact(value):
     high = value.astype(jnp.bfloat16)
     low = (value - high.astype(jnp.float32)).astype(jnp.bfloat16)
@@ -185,9 +162,11 @@
     return lax.dot_general(select, value, (((1,), (1,)), ((), ())), preferred_element_type=jnp.float32)
 
 
-def pair_kernel(groups, idx_ref, win_ref, bins_ref, out_ref, wide, own_tile, turned, places, arrived, *tiles):
+def pair_part(groups, idx_ref, win_ref, vwin_ref, bins_ref, out_ref, cos_buf, sin_buf, real_buf, imag_buf, root_buf,
+              wide, own_tile, turned, places, arrived, tiles):
     rows = win_ref.shape[1]
-    fetch = lambda group, at: pltpu.make_async_copy(idx_ref.at[group], places[at], arrived.at[at])
+    eight = lambda group: pl.ds(group * 8 if isinstance(group, int) else pl.multiple_of(group * 8, 8), 8)
+    fetch = lambda group, at: pltpu.make_async_copy(idx_ref.at[eight(group)], places[at], arrived.at[at])
     fetch(0, 0).start()
     fetch(1, 1).start()
     first = lax.axis_index("freq") * (LANES // (2 * RADIAL))
@@ -199,7 +178,10 @@
 
     for block in range(BLOCKS):
         wide[block * rows:(block + 1) * rows, :] = win_ref[block].astype(jnp.float32)
-    own = win_ref[lax.rem(lax.axis_index("img"), 8)].astype(jnp.float32)
+    here = lax.rem(lax.axis_index("img"), 8)
+    own = win_ref[here].astype(jnp.float32)
+    own_sq = vwin_ref[here]
+    own_root = lax.rsqrt(jnp.where(line % 2 == 0, own_sq[4:5], own_sq[5:6]) + norm_eps)
     own_tile[...] = own
     column = lax.broadcasted_iota(jnp.int32, own.shape, 1)
     turned[...] = jnp.where(column % (2 * RADIAL) < RADIAL,
@@ -216,13 +198,22 @@
         if then is not None:
             fetch(then, at).start()
         result = jnp.zeros((8, LANES), jnp.float32)
+        spots = idx_ref[eight(group), :]
+        spins = bins_ref[eight(group), :].astype(jnp.float32)
+        ((real, imag, square),) = pick([spots & (LANES - 1)], [spots >> 7], vwin_ref, (0, 2, 4))
+        cos, sin = cos_sin_turns(spins)
+        cos_buf[group] = cos
+        sin_buf[group] = sin
+        real_buf[group] = cos * real - sin * imag
+        imag_buf[group] = sin * real + cos * imag
+        root_buf[group] = lax.rsqrt(square + norm_eps) * own_root
         for n in range(8):
             half = slice((n % 2) * LANES, (n % 2 + 1) * LANES)
             other = tiles[n][...]
             real = split_exact(own_tile[half, :] * other)
             imag = split_exact(turned[half, :] * other)
             sums = lane_sums(select, jnp.concatenate([real, imag], axis=0))
-            units = bins_ref[group, n:n + 1, :].astype(jnp.float32) * freq
+            units = spins[n:n + 1, :] * freq
             cos, sin = cos_sin_turns(units)
             terms = sums[:, :LANES] * cos - sums[:, LANES:] * sin
             result = jnp.where(line == n, jnp.sum(terms, axis=0, keepdims=True), result)
@@ -236,24 +227,6 @@
     lax.fori_loop(0, groups // 2, body, 0)
     one_group(groups - 1, 0)
     fetch(groups - 1, 1).wait()
-
-
-def pair_call(idx, window, bins):
-    blocks, rows, width = window.shape
-    groups = idx.shape[0]
-    vmem = pl.BlockSpec(memory_space=pltpu.VMEM)
-    return pl.pallas_call(
-        lambda *refs: pair_kernel(groups, *refs[:7], refs[7:9], *refs[9:]),
-        out_shape=jax.ShapeDtypeStruct((16, 8, LANES), jnp.float32),
-        in_specs=[pl.BlockSpec(memory_space=pl.ANY), vmem, vmem],
-        out_specs=vmem,
-        scratch_shapes=[pltpu.VMEM((blocks * rows, width), jnp.float32),
-                        pltpu.VMEM((rows, width), jnp.float32), pltpu.VMEM((rows, width), jnp.float32),
-                        pltpu.SMEM((8, LANES), jnp.int32), pltpu.SMEM((8, LANES), jnp.int32),
-                        pltpu.SemaphoreType.DMA((2,))]
-        + [pltpu.VMEM((LANES, LANES), jnp.float32)] * 8,
-        name="pairs",
-    )(idx, window, bins)
 
 
 def pick(low, high, ref, lines):
@@ -276,61 +249,45 @@
     return total + pltpu.roll(total, 2, 0)
 
 
-def power_kernel(count, groups, part_ref, vwin_ref, idx_ref, bins_ref, deg_ref, weights_ref, vec_ref,
-                 cos_buf, sin_buf, real_buf, imag_buf, root_buf, rs_buf, ag_buf, vec1, vec2, ynorm, znorm,
-                 rs_send, rs_recv, ag_send, ag_recv, v_send, v_recv, n_send, n_recv):
+def power_part(count, groups, part_ref, idx_ref, deg_ref, weights_ref, vec_ref,
+               cos_buf, sin_buf, real_buf, imag_buf, root_buf, rs_buf, ag_buf, vec1, vec2, ynorm, znorm,
+               rs_send, rs_recv, ag_send, ag_recv, v_send, v_recv, n_send, n_recv):
     me = lax.axis_index("img")
     mine = lax.axis_index("freq")
     y, z = lax.rem(me, 8), lax.div(me, 8)
     freq_at = lambda q: {"freq": lax.rem(mine + q, 8)}
     y_at, z_at = ring(me, z, y)
-    met = greet([img_at(me, step, count) for step in STEPS] + [freq_at(q) for q in range(1, 8)]
-                + [y_at(q) for q in range(1, 8)] + [z_at(q) for q in range(1, 8)])
-    sub = lax.broadcasted_iota(jnp.int32, (8, LANES), 0)
-    degree = jnp.where(sub % 2 == 0, deg_ref[0:1, :], deg_ref[1:2, :])
-    low = [idx_ref[m * 8:(m + 1) * 8, :] & (LANES - 1) for m in range(groups)]
-    high = [idx_ref[m * 8:(m + 1) * 8, :] >> 7 for m in range(groups)]
-    own_sq = vwin_ref[y]
-    own_root = lax.rsqrt(jnp.where(sub % 2 == 0, own_sq[4:5], own_sq[5:6]) + norm_eps)
-    for m, (real, imag, square) in enumerate(pick(low, high, vwin_ref, (0, 2, 4))):
-        cos, sin = cos_sin_turns(bins_ref[m * 8:(m + 1) * 8, :].astype(jnp.float32))
-        cos_buf[m] = cos
-        sin_buf[m] = sin
-        real_buf[m] = cos * real - sin * imag
-        imag_buf[m] = sin * real + cos * imag
-        root_buf[m] = lax.rsqrt(square + norm_eps) * own_root
-    met()
-
+    two = lambda piece: pl.ds(2 * piece, 2)
     copies = []
     for q in range(1, 8):
         copy = pltpu.make_async_remote_copy(
-            src_ref=part_ref.at[lax.rem(mine + q, 8)], dst_ref=rs_buf.at[q - 1],
+            src_ref=part_ref.at[two(lax.rem(mine + q, 8))], dst_ref=rs_buf.at[q - 1],
             send_sem=rs_send.at[q - 1], recv_sem=rs_recv.at[q - 1], device_id=freq_at(q), device_id_type=MESH)
         copy.start()
         copies.append(copy)
     for copy in copies:
         copy.wait()
-    total = part_ref[mine]
+    total = part_ref[two(mine)]
     for q in range(7):
         total = total + rs_buf[q]
-    ag_buf[mine] = total
+    ag_buf[two(mine)] = total
     copies = []
     for q in range(1, 8):
         copy = pltpu.make_async_remote_copy(
-            src_ref=ag_buf.at[mine], dst_ref=ag_buf.at[mine],
+            src_ref=ag_buf.at[two(mine)], dst_ref=ag_buf.at[two(mine)],
             send_sem=ag_send.at[q - 1], recv_sem=ag_recv.at[q - 1], device_id=freq_at(q), device_id_type=MESH)
         copy.start()
         copies.append(copy)
     for copy in copies:
         copy.wait()
 
-    def ag_row(row, size):
-        piece, at = row // PIECE, row % PIECE
-        return ag_buf[piece, at:at + size, :]
-
+    sub = lax.broadcasted_iota(jnp.int32, (8, LANES), 0)
+    degree = jnp.where(sub % 2 == 0, deg_ref[0:1, :], deg_ref[1:2, :])
+    low = [idx_ref[m * 8:(m + 1) * 8, :] & (LANES - 1) for m in range(groups)]
+    high = [idx_ref[m * 8:(m + 1) * 8, :] >> 7 for m in range(groups)]
     denom = jnp.zeros((8, LANES), jnp.float32)
     for m in range(groups):
-        cos_sim = ag_row(m * 8, 8) * root_buf[m]
+        cos_sim = ag_buf[m] * root_buf[m]
         raw = jnp.where((sub // 2 + m * 4) < degree, jnp.exp(sharpness * cos_sim), 0.0)
         weights_ref[m * 8:(m + 1) * 8, :] = raw
         denom = denom + raw
@@ -401,31 +358,52 @@
             vec_ref[part:part + 1, lanes] = packed_ref[part * 2 + half:part * 2 + half + 1, :]
 
 
-def power_call(part, vwin, idx, bins, deg, count):
-    groups = idx.shape[0] // 8
+def whole_call(coef, neighbours, rot_bin, deg, v_init, count):
+    rows, width = coef.shape
+    groups = TALL // 8
+    n = len(STEPS)
     vmem = pl.BlockSpec(memory_space=pltpu.VMEM)
-    n = len(STEPS)
     dma = pltpu.SemaphoreType.DMA
+    real = lambda *shape: pltpu.VMEM(shape, jnp.float32)
+    window = [pltpu.VMEM((BLOCKS, rows, width), coef.dtype), real(BLOCKS, 8, LANES),
+              pltpu.VMEM((TALL, LANES), jnp.int32), pltpu.VMEM((TALL, LANES), jnp.int32),
+              real(8, LANES), real(8, 8, LANES), dma((2, 4, 2)), dma((2, 4, 2)), dma((9, 2)), dma((9, 2)),
+              dma((n,)), dma((n,)), dma((7,)), dma((7,)), dma((1,))]
+    shared = [real(16, 8, LANES)] + [real(groups, 8, LANES)] * 5
+    pairs = [real(BLOCKS * rows, width), real(rows, width), real(rows, width), pltpu.SMEM((8, LANES), jnp.int32),
+             pltpu.SMEM((8, LANES), jnp.int32), dma((2,))] + [real(LANES, LANES)] * 8
+    power = [real(7, 2, 8, LANES), real(16, 8, LANES), real(BLOCKS, 8, LANES), real(BLOCKS, 8, LANES),
+             real(8, 8, LANES), real(8, 8, LANES),
+             dma((7,)), dma((7,)), dma((7,)), dma((7,)), dma((2, n)), dma((2, n)), dma((2, 7)), dma((2, 7))]
+
+    def kernel(coef_ref, nei_ref, bin_ref, deg_ref, v_ref, weights_ref, vec_ref, *scratch):
+        me = lax.axis_index("img")
+        mine = lax.axis_index("freq")
+        y_at, z_at = ring(me, lax.div(me, 8), lax.rem(me, 8))
+        met = greet([img_at(me, step, count) for step in STEPS] + [{"freq": lax.rem(mine + q, 8)} for q in range(1, 8)]
+                    + [y_at(q) for q in range(1, 8)] + [z_at(q) for q in range(1, 8)])
+        cut = [0]
+        for part in (window, shared, pairs, power):
+            cut.append(cut[-1] + len(part))
+        win, both, pair, last = [scratch[a:b] for a, b in zip(cut, cut[1:])]
+        window_part(count, met, coef_ref, nei_ref, bin_ref, v_ref, *win)
+        pair_part(groups, win[2], win[0], win[1], win[3], *both, *pair[:3], pair[3:5], pair[5], pair[6:])
+        power_part(count, groups, both[0], win[2], deg_ref, weights_ref, vec_ref, *both[1:], *last)
+
     return pl.pallas_call(
-        lambda *refs: power_kernel(count, groups, *refs),
-        out_shape=(jax.ShapeDtypeStruct(idx.shape, jnp.float32), jax.ShapeDtypeStruct((8, LANES), jnp.float32)),
+        kernel,
+        out_shape=(jax.ShapeDtypeStruct((TALL, LANES), jnp.float32), jax.ShapeDtypeStruct((8, LANES), jnp.float32)),
         in_specs=[vmem] * 5,
         out_specs=(vmem, vmem),
-        scratch_shapes=[pltpu.VMEM((groups, 8, LANES), jnp.float32)] * 5 + [pltpu.VMEM((7, PIECE, LANES), jnp.float32), pltpu.VMEM((8, PIECE, LANES), jnp.float32),
-                        pltpu.VMEM((BLOCKS, 8, LANES), jnp.float32), pltpu.VMEM((BLOCKS, 8, LANES), jnp.float32),
-                        pltpu.VMEM((8, 8, LANES), jnp.float32), pltpu.VMEM((8, 8, LANES), jnp.float32),
-                        dma((7,)), dma((7,)), dma((7,)), dma((7,)), dma((2, n)), dma((2, n)), dma((2, 7)), dma((2, 7))],
-        compiler_params=pltpu.CompilerParams(collective_id=1, has_side_effects=True),
-        name="power",
-    )(part, vwin, idx, bins, deg)
+        scratch_shapes=window + shared + pairs + power,
+        compiler_params=pltpu.CompilerParams(collective_id=0, has_side_effects=True),
+        name="whole",
+    )(coef, neighbours, rot_bin, deg, v_init)
 
 
 def shards(coef, neighbours, rot_bin, degree, v_init):
     count = lax.axis_size("img")
-    window, vwin, idx, bins = window_call(coef, neighbours, rot_bin, v_init, count)
-    groups = lambda value: value.reshape(TALL // 8, 8, LANES)
-    part = pair_call(groups(idx), window, groups(bins))
-    tall, packed = power_call(part.reshape(8, PIECE, LANES), vwin, idx, bins, degree.reshape(2, LANES), count)
+    tall, packed = whole_call(coef, neighbours, rot_bin, degree.reshape(2, LANES), v_init, count)
     vmem = pl.BlockSpec(memory_space=pltpu.VMEM)
     weights, vector = pl.pallas_call(
         finish_kernel,

time: 88.7 us -> 80.8 us (0.911)
  Pallas kernels: 87.7 us -> 79.9 us
    pallas_call x3 -> x1, Pallas kernels: 86.3 us -> 78.5 us  [whole_call(): pl.pallas_call(kernel, out_shape=(jax.ShapeDtypeStruct((TALL, LANES), jnp...]
where the time goes in v5:
time: 80.8 us; the launch traced here: 80.6 us
  Pallas kernels  79.9 us (99%)
    pallas_call x1, Pallas kernels, whole_call(): pl.pallas_call(kernel, out_shape=(jax.ShapeDtypeStruct((TALL, LANES), jnp...  78.5 us

profile of v5, /device:TPU:2, one launch (start us, length us, event | category | flops | bytes accessed | tf_op | source)
XLA Modules:
  0.0 80.6 jit_solution(9925880312707490366)
XLA Ops:
  0.6 78.5 %whole.1 = (f32[104,128]{1,0:T(8,128)}, f32[8,128]{1,0:T(8,128)}) custom-call(bf16[256,128]{1,0:T(8,128)(2,1)} %coef_ref.1, s32[50,256]{1,0:T(8,128)} %nei_ref.1, s32[50,256]{1,0:T(8,128)} %bin_ref.1, s32[2,128]{1,0:T(2,128)} %bitcast.1, f32[2,256]{1,0:T(2,128)} %v_ref.1), custom_call_target="tpu_custom_call" | custom-call | tf_op jit(solution)/shard_map/whole/pallas_call | solution.py:393
  79.1 1.4 %finish.1 = (f32[50,256]{1,0:T(8,128)}, f32[2,256]{1,0:T(2,128)}) custom-call(f32[104,128]{1,0:T(8,128)} %get-tuple-element.6.tall_ref, f32[8,128]{1,0:T(8,128)} %get-tuple-element.7.packed_ref), custom_call_target="tpu_custom_call" | custom-call | tf_op jit(solution)/shard_map/finish/pallas_call | solution.py:408

commit v6 on v5

--- a/solution.py
+++ b/solution.py
@@ -63,15 +63,20 @@
     return mine_y + SPAN * row * row
 
 
-def window_part(count, met, coef_ref, nei_ref, bin_ref, v_ref, win_ref, vwin_ref, idx_ref, bins_ref, message, squares,
-                y_send, y_recv, z_send, z_recv, v_send, v_recv, s_send, s_recv, local):
+def window_part(count, met, coef_ref, nei_ref, bin_ref, v_ref, wide, win_ref, vwin_ref, idx_ref, bins_ref, message,
+                squares,                y_send, y_recv, z_send, z_recv, v_send, v_recv, s_send, s_recv):
     me = lax.axis_index("img")
     mine = lax.axis_index("freq")
     y, z = lax.rem(me, 8), lax.div(me, 8)
     y_at, z_at = ring(me, z, y)
     freq_at = lambda q: {"freq": lax.rem(mine + q, 8)}
-    own = pltpu.make_async_copy(coef_ref, win_ref.at[y], local.at[0])
-    own.start()
+    images = coef_ref.shape[0]
+
+    def widen(slot, value):
+        start = slot * images if isinstance(slot, int) else pl.multiple_of(slot * images, images)
+        wide[pl.ds(start, images), :] = value.astype(jnp.float32)
+
+    widen(y, coef_ref[...])
     ones = jnp.ones((8, 2 * LANES), jnp.bfloat16)
     for half in range(2):
         piece = coef_ref[half * LANES:(half + 1) * LANES, :].astype(jnp.float32)
@@ -90,14 +95,17 @@
 
     ways = (1, 7)
     chunk = lambda c: pl.ds(c * LANES, LANES)
-    flows, rows = {}, []
+    flows, rows, landed = {}, [], {7: 8 + y, 8: 16}
+    across = {at: [] for at in range(9)}
     for c in range(2):
         for w in range(2):
             flows[w, 0, c] = send(coef_ref.at[chunk(c)], win_ref.at[y, chunk(c)], y_send.at[w, 0, c],
                                   y_recv.at[w, 0, c], y_at(ways[w]))
     for c in range(2):
-        rows.append(send(coef_ref.at[chunk(c)], win_ref.at[8 + y, chunk(c)], z_send.at[7, c], z_recv.at[7, c], z_at(1)))
-        rows.append(send(coef_ref.at[chunk(c)], win_ref.at[16, chunk(c)], z_send.at[8, c], z_recv.at[8, c], z_at(7)))
+        across[7].append(send(coef_ref.at[chunk(c)], win_ref.at[8 + y, chunk(c)], z_send.at[7, c], z_recv.at[7, c],
+                              z_at(1)))
+        across[8].append(send(coef_ref.at[chunk(c)], win_ref.at[16, chunk(c)], z_send.at[8, c], z_recv.at[8, c],
+                              z_at(7)))
     sums = [send(squares.at[mine], squares.at[mine], s_send.at[q - 1], s_recv.at[q - 1], freq_at(q))
             for q in range(1, 8)]
 
@@ -128,8 +136,14 @@
                 if q < 3 or (q == 3 and w == c):
                     flows[w, q, c] = send(held, held, y_send.at[w, q, c], y_recv.at[w, q, c], y_at(ways[w]))
                 at = (q - 1) * 2 + w if q < 4 else 6
-                rows.append(send(held, win_ref.at[8 + block_at, chunk(c)], z_send.at[at, c], z_recv.at[at, c],
-                                 z_at(1 + 6 * turn)))
+                across[at].append(send(held, win_ref.at[8 + block_at, chunk(c)], z_send.at[at, c], z_recv.at[at, c],
+                                       z_at(1 + 6 * turn)))
+                landed[at] = 8 + block_at
+                if c == 1:
+                    rows.append(block_at)
+        while rows:
+            slot = rows.pop()
+            widen(slot, win_ref[slot])
         if q == 1:
             for copy in sums:
                 copy.wait()
@@ -145,11 +159,14 @@
             vwin_ref[y] = packed
             small = [send(message, vwin_ref.at[landing_slot(y, step)], v_send.at[n], v_recv.at[n],
                           img_at(me, step, count)) for n, step in enumerate(STEPS)]
-    for copy in small + rows:
+    for at in (7, 8, 0, 1, 2, 3, 4, 5, 6):
+        for copy in across[at]:
+            copy.wait()
+        widen(landed[at], win_ref[landed[at]])
+    for copy in small:
         copy.wait()
     for copy in flows.values():
         copy.wait_send()
-    own.wait()
 
 
 def split_exact(value):
@@ -162,9 +179,8 @@
     return lax.dot_general(select, value, (((1,), (1,)), ((), ())), preferred_element_type=jnp.float32)
 
 
-def pair_part(groups, idx_ref, win_ref, vwin_ref, bins_ref, out_ref, cos_buf, sin_buf, real_buf, imag_buf, root_buf,
+def pair_part(groups, idx_ref, coef_ref, vwin_ref, bins_ref, out_ref, cos_buf, sin_buf, real_buf, imag_buf, root_buf,
               wide, own_tile, turned, places, arrived, tiles):
-    rows = win_ref.shape[1]
     eight = lambda group: pl.ds(group * 8 if isinstance(group, int) else pl.multiple_of(group * 8, 8), 8)
     fetch = lambda group, at: pltpu.make_async_copy(idx_ref.at[eight(group)], places[at], arrived.at[at])
     fetch(0, 0).start()
@@ -176,10 +192,8 @@
     freq = (first + lax.broadcasted_iota(jnp.int32, (8, LANES), 0)).astype(jnp.float32)
     line = lax.broadcasted_iota(jnp.int32, (8, LANES), 0)
 
-    for block in range(BLOCKS):
-        wide[block * rows:(block + 1) * rows, :] = win_ref[block].astype(jnp.float32)
     here = lax.rem(lax.axis_index("img"), 8)
-    own = win_ref[here].astype(jnp.float32)
+    own = coef_ref[...].astype(jnp.float32)
     own_sq = vwin_ref[here]
     own_root = lax.rsqrt(jnp.where(line % 2 == 0, own_sq[4:5], own_sq[5:6]) + norm_eps)
     own_tile[...] = own
@@ -192,32 +206,34 @@
     def one_group(group, at, then=None):
         fetch(group, at).wait()
         place = places[at]
-        for n in range(8):
-            for pair in range(LANES):
-                tiles[n][pair:pair + 1, :] = wide[pl.ds(place[n, pair], 1), :]
-        if then is not None:
-            fetch(then, at).start()
-        result = jnp.zeros((8, LANES), jnp.float32)
         spots = idx_ref[eight(group), :]
         spins = bins_ref[eight(group), :].astype(jnp.float32)
-        ((real, imag, square),) = pick([spots & (LANES - 1)], [spots >> 7], vwin_ref, (0, 2, 4))
-        cos, sin = cos_sin_turns(spins)
-        cos_buf[group] = cos
-        sin_buf[group] = sin
-        real_buf[group] = cos * real - sin * imag
-        imag_buf[group] = sin * real + cos * imag
-        root_buf[group] = lax.rsqrt(square + norm_eps) * own_root
-        for n in range(8):
-            half = slice((n % 2) * LANES, (n % 2 + 1) * LANES)
-            other = tiles[n][...]
+        result = jnp.zeros((8, LANES), jnp.float32)
+        for n in range(9):
+            if n < 8:
+                for pair in range(LANES):
+                    tiles[n][pair:pair + 1, :] = wide[pl.ds(place[n, pair], 1), :]
+            if n == 0:
+                ((real, imag, square),) = pick([spots & (LANES - 1)], [spots >> 7], vwin_ref, (0, 2, 4))
+                cos, sin = cos_sin_turns(spins)
+                cos_buf[group] = cos
+                sin_buf[group] = sin
+                real_buf[group] = cos * real - sin * imag
+                imag_buf[group] = sin * real + cos * imag
+                root_buf[group] = lax.rsqrt(square + norm_eps) * own_root
+                continue
+            done = n - 1
+            half = slice((done % 2) * LANES, (done % 2 + 1) * LANES)
+            other = tiles[done][...]
             real = split_exact(own_tile[half, :] * other)
             imag = split_exact(turned[half, :] * other)
             sums = lane_sums(select, jnp.concatenate([real, imag], axis=0))
-            units = spins[n:n + 1, :] * freq
-            cos, sin = cos_sin_turns(units)
+            cos, sin = cos_sin_turns(spins[done:done + 1, :] * freq)
             terms = sums[:, :LANES] * cos - sums[:, LANES:] * sin
-            result = jnp.where(line == n, jnp.sum(terms, axis=0, keepdims=True), result)
+            result = jnp.where(line == done, jnp.sum(terms, axis=0, keepdims=True), result)
         out_ref[group] = result
+        if then is not None:
+            fetch(then, at).start()
 
     def body(step, carry):
         one_group(2 * step, 0, 2 * step + 2)
@@ -368,7 +384,7 @@
     window = [pltpu.VMEM((BLOCKS, rows, width), coef.dtype), real(BLOCKS, 8, LANES),
               pltpu.VMEM((TALL, LANES), jnp.int32), pltpu.VMEM((TALL, LANES), jnp.int32),
               real(8, LANES), real(8, 8, LANES), dma((2, 4, 2)), dma((2, 4, 2)), dma((9, 2)), dma((9, 2)),
-              dma((n,)), dma((n,)), dma((7,)), dma((7,)), dma((1,))]
+              dma((n,)), dma((n,)), dma((7,)), dma((7,))]
     shared = [real(16, 8, LANES)] + [real(groups, 8, LANES)] * 5
     pairs = [real(BLOCKS * rows, width), real(rows, width), real(rows, width), pltpu.SMEM((8, LANES), jnp.int32),
              pltpu.SMEM((8, LANES), jnp.int32), dma((2,))] + [real(LANES, LANES)] * 8
@@ -386,8 +402,8 @@
         for part in (window, shared, pairs, power):
             cut.append(cut[-1] + len(part))
         win, both, pair, last = [scratch[a:b] for a, b in zip(cut, cut[1:])]
-        window_part(count, met, coef_ref, nei_ref, bin_ref, v_ref, *win)
-        pair_part(groups, win[2], win[0], win[1], win[3], *both, *pair[:3], pair[3:5], pair[5], pair[6:])
+        window_part(count, met, coef_ref, nei_ref, bin_ref, v_ref, pair[0], *win)
+        pair_part(groups, win[2], coef_ref, win[1], win[3], *both, *pair[:3], pair[3:5], pair[5], pair[6:])
         power_part(count, groups, both[0], win[2], deg_ref, weights_ref, vec_ref, *both[1:], *last)
 
     return pl.pallas_call(

time: 80.8 us -> 80.9 us (level)
  no operation moved by 1% of the time
where the time goes in v6:
time: 80.9 us; the launch traced here: 80.7 us
  Pallas kernels  80 us (99%)
    pallas_call x1, Pallas kernels, whole_call(): pl.pallas_call(kernel, out_shape=(jax.ShapeDtypeStruct((TALL, LANES), jnp...  78.6 us

profile of v6, /device:TPU:2, one launch (start us, length us, event | category | flops | bytes accessed | tf_op | source)
XLA Modules:
  0.0 80.7 jit_solution(5654853214912262819)
XLA Ops:
  0.6 78.6 %whole.1 = (f32[104,128]{1,0:T(8,128)}, f32[8,128]{1,0:T(8,128)}) custom-call(bf16[256,128]{1,0:T(8,128)(2,1)} %coef_ref.1, s32[50,256]{1,0:T(8,128)} %nei_ref.1, s32[50,256]{1,0:T(8,128)} %bin_ref.1, s32[2,128]{1,0:T(2,128)} %bitcast.1, f32[2,256]{1,0:T(2,128)} %v_ref.1), custom_call_target="tpu_custom_call" | custom-call | tf_op jit(solution)/shard_map/whole/pallas_call | solution.py:409
  79.2 1.4 %finish.1 = (f32[50,256]{1,0:T(8,128)}, f32[2,256]{1,0:T(2,128)}) custom-call(f32[104,128]{1,0:T(8,128)} %get-tuple-element.6.tall_ref, f32[8,128]{1,0:T(8,128)} %get-tuple-element.7.packed_ref), custom_call_target="tpu_custom_call" | custom-call | tf_op jit(solution)/shard_map/finish/pallas_call | solution.py:424

commit v7 on v5

--- a/solution.py
+++ b/solution.py
@@ -89,13 +89,14 @@
         return copy
 
     ways = (1, 7)
-    chunk = lambda c: pl.ds(c * LANES, LANES)
+    quarter = coef_ref.shape[0] // 4
+    chunk = lambda c: pl.ds(c * quarter, quarter)
     flows, rows = {}, []
-    for c in range(2):
+    for c in range(4):
         for w in range(2):
             flows[w, 0, c] = send(coef_ref.at[chunk(c)], win_ref.at[y, chunk(c)], y_send.at[w, 0, c],
                                   y_recv.at[w, 0, c], y_at(ways[w]))
-    for c in range(2):
+    for c in range(4):
         rows.append(send(coef_ref.at[chunk(c)], win_ref.at[8 + y, chunk(c)], z_send.at[7, c], z_recv.at[7, c], z_at(1)))
         rows.append(send(coef_ref.at[chunk(c)], win_ref.at[16, chunk(c)], z_send.at[8, c], z_recv.at[8, c], z_at(7)))
     sums = [send(squares.at[mine], squares.at[mine], s_send.at[q - 1], s_recv.at[q - 1], freq_at(q))
@@ -115,9 +116,9 @@
 
     small = []
     for q in range(1, 5):
-        for c in range(2):
+        for c in range(4):
             for w in range(2):
-                if q == 4 and w != c:
+                if q == 4 and w != c // 2:
                     continue
                 block_at = lax.rem(y + (8 - q if w == 0 else q), 8)
                 turn = lax.div(y - q + 8, 8) if w == 0 else lax.div(y + q, 8)
@@ -125,7 +126,7 @@
                     turn = lax.div(y + 4, 8)
                 flows[w, q - 1, c].wait_recv()
                 held = win_ref.at[block_at, chunk(c)]
-                if q < 3 or (q == 3 and w == c):
+                if q < 3 or (q == 3 and w == c // 2):
                     flows[w, q, c] = send(held, held, y_send.at[w, q, c], y_recv.at[w, q, c], y_at(ways[w]))
                 at = (q - 1) * 2 + w if q < 4 else 6
                 rows.append(send(held, win_ref.at[8 + block_at, chunk(c)], z_send.at[at, c], z_recv.at[at, c],
@@ -367,7 +368,7 @@
     real = lambda *shape: pltpu.VMEM(shape, jnp.float32)
     window = [pltpu.VMEM((BLOCKS, rows, width), coef.dtype), real(BLOCKS, 8, LANES),
               pltpu.VMEM((TALL, LANES), jnp.int32), pltpu.VMEM((TALL, LANES), jnp.int32),
-              real(8, LANES), real(8, 8, LANES), dma((2, 4, 2)), dma((2, 4, 2)), dma((9, 2)), dma((9, 2)),
+              real(8, LANES), real(8, 8, LANES), dma((2, 4, 4)), dma((2, 4, 4)), dma((9, 4)), dma((9, 4)),
               dma((n,)), dma((n,)), dma((7,)), dma((7,)), dma((1,))]
     shared = [real(16, 8, LANES)] + [real(groups, 8, LANES)] * 5
     pairs = [real(BLOCKS * rows, width), real(rows, width), real(rows, width), pltpu.SMEM((8, LANES), jnp.int32),

time: 80.8 us -> 80.7 us (level)
  the two profiles are of different devices: /device:TPU:2 before, /device:TPU:8 now
where the time goes in v7:
time: 80.7 us; the launch traced here: 80.5 us
  Pallas kernels  79.9 us (99%)
    pallas_call x1, Pallas kernels, whole_call(): pl.pallas_call(kernel, out_shape=(jax.ShapeDtypeStruct((TALL, LANES), jnp...  78.4 us

profile of v7, /device:TPU:8, one launch (start us, length us, event | category | flops | bytes accessed | tf_op | source)
XLA Modules:
  0.0 80.5 jit_solution(8243372469950657718)
XLA Ops:
  0.6 78.4 %whole.1 = (f32[104,128]{1,0:T(8,128)}, f32[8,128]{1,0:T(8,128)}) custom-call(bf16[256,128]{1,0:T(8,128)(2,1)} %coef_ref.1, s32[50,256]{1,0:T(8,128)} %nei_ref.1, s32[50,256]{1,0:T(8,128)} %bin_ref.1, s32[2,128]{1,0:T(2,128)} %bitcast.1, f32[2,256]{1,0:T(2,128)} %v_ref.1), custom_call_target="tpu_custom_call" | custom-call | tf_op jit(solution)/shard_map/whole/pallas_call | solution.py:394
  79.1 1.4 %finish.1 = (f32[50,256]{1,0:T(8,128)}, f32[2,256]{1,0:T(2,128)}) custom-call(f32[104,128]{1,0:T(8,128)} %get-tuple-element.6.tall_ref, f32[8,128]{1,0:T(8,128)} %get-tuple-element.7.packed_ref), custom_call_target="tpu_custom_call" | custom-call | tf_op jit(solution)/shard_map/finish/pallas_call | solution.py:409
